TPU v7x, 256 devices: a whole 4x4x8 slice. The times are simulated.
256 devices in a mesh: depth: 64 (over y, z, core), xr: 4 (over x).
Axes of the slice: x: 4, y: 4, z: 8, core: 2. Of those that a mesh axis runs over, the one named last changes fastest.
Arguments:
- sound_field: float32 [2, 4096, 3584], P(None, 'depth', 'xr'), may hold values from -6 to 6
- index_start: float32 [4096, 3584], P('depth', 'xr'), may hold values from 0.8 to 0.98
- index_end: float32 [4096, 3584], P('depth', 'xr'), may hold values from 0.8 to 0.98
Outputs:
- stepped: float32 [2, 4096, 3584], P(None, ('depth', 'xr'))
All inputs are finite; a program needn't handle non-finite values.
Results may differ from a plain program's by a relative error of at most 0.00035.
Values sent between devices are 32-bit elements; how exact they have to be, the bound alone decides.
No kernel may reach another device: no remote copies, remote signals or barrier semaphores. Data moves between devices by JAX's collectives and lax.ppermute only.
A program may use at most 128 MiB of HBM per device.

v0:
```python
import jax
import jax.numpy as jnp
from jax import lax
from jax.experimental import pallas as pl
from jax.experimental.pallas import tpu as pltpu
from jax.sharding import Mesh
from jax.sharding import PartitionSpec as P

DEPTH = ("y", "z", "c")

DEPTH_STIFFNESS = 1.6
CROSS_STIFFNESS = 1.2
NUMER = complex(2.857, 0.004)
DENOM = complex(2.857, -0.004)

MIX = NUMER / DENOM

SUB = 8
LANE = 128
CELLS = 64
PARTS = 12


def constants(stiffness):
    slope = -0.5 / stiffness
    base = 2.0 - (1.0 / DENOM).real / stiffness - slope
    swing = -(1.0 / DENOM).imag / stiffness
    gain = (1.0 - MIX) / (stiffness * DENOM)
    return base, slope, swing, gain


def mul(a, b):
    return a[0] * b[0] - a[1] * b[1], a[0] * b[1] + a[1] * b[0]


def add(a, b):
    return a[0] + b[0], a[1] + b[1]


def sub(a, b):
    return a[0] - b[0], a[1] - b[1]


def scaled(a, s):
    return a[0] * s, a[1] * s


def pick(flag, yes, no):
    return [(jnp.where(flag, p[0], q[0]), jnp.where(flag, p[1], q[1])) for p, q in zip(yes, no)]


def compose(early, late):
    a00, a10, a01, a11, r0, r1 = early
    b00, b10, b01, b11, s0, s1 = late
    return [
        add(mul(b00, a00), mul(b01, a10)),
        add(mul(b10, a00), mul(b11, a10)),
        add(mul(b00, a01), mul(b01, a11)),
        add(mul(b10, a01), mul(b11, a11)),
        add(r0, add(mul(a00, s0), mul(a10, s1))),
        add(r1, add(mul(a01, s0), mul(a11, s1))),
    ]


def normal(state):
    f0, f1, g = state
    size = jnp.maximum(
        jnp.maximum(jnp.abs(f0[0]), jnp.abs(f0[1])), jnp.maximum(jnp.abs(f1[0]), jnp.abs(f1[1]))
    )
    scale = 1.0 / size
    return [scaled(f0, scale), scaled(f1, scale), scaled(g, scale)]


def advance(state, span):
    f0, f1, g = state
    t00, t10, t01, t11, s0, s1 = span
    return [
        add(mul(t00, f0), mul(t01, f1)),
        add(mul(t10, f0), mul(t11, f1)),
        add(g, add(mul(f0, s0), mul(f1, s1))),
    ]


def retreat(state, span):
    p0, p1, h = state
    t00, t10, t01, t11, s0, s1 = span
    q0 = sub(mul(t11, p0), mul(t01, p1))
    q1 = sub(mul(t00, p1), mul(t10, p0))
    return [q0, q1, add(h, add(mul(q0, s0), mul(q1, s1)))]


def meet(left, right):
    f0, f1, g = left
    p0, p1, h = right
    det = sub(mul(f1, p0), mul(f0, p1))
    scale = -1.0 / (det[0] * det[0] + det[1] * det[1])
    inverse = (det[0] * scale, -det[1] * scale)
    v0 = mul(add(mul(f0, h), mul(p0, g)), inverse)
    v1 = mul(add(mul(g, p1), mul(f1, h)), inverse)
    return v0, v1


def ends(like):
    zero = jnp.zeros_like(like)
    one = zero + 1.0
    return [(zero, zero), (one, zero), (zero, zero)], [(one, zero), (zero, zero), (zero, zero)]


def read(ref):
    return [(ref[2 * i], ref[2 * i + 1]) for i in range(PARTS // 2)]


def write(ref, span):
    for i, part in enumerate(span):
        ref[2 * i] = part[0]
        ref[2 * i + 1] = part[1]


def rows(k):
    return pl.ds(SUB * k, SUB)


def march_span(source, curve, swing, every=CELLS):
    zero = jnp.zeros((SUB, LANE), jnp.float32)
    one = zero + 1.0
    past = [(one, zero), (zero, zero)]
    now = [(zero, zero), (one, zero)]
    sums = [(zero, zero), (zero, zero)]
    spans = []
    for k in range(CELLS):
        u = source[0, rows(k), :], source[1, rows(k), :]
        c = curve[rows(k), :]
        for i in range(2):
            p, n = past[i], now[i]
            sums[i] = add(sums[i], mul(n, u))
            new = (c * n[0] - (swing * n[1] + p[0]), c * n[1] + (swing * n[0] - p[1]))
            past[i], now[i] = n, new
        if (k + 1) % every == 0:
            spans.append([past[0], now[0], past[1], now[1], sums[0], sums[1]])
    return spans


def march_solution(source, curve, swing, gain, v0, v1, target, count=CELLS):
    past, now = v0, v1
    for k in range(count):
        u, c = source(k), curve(k)
        target(
            k,
            (MIX.real * u[0] - MIX.imag * u[1]) + (gain.real * now[0] - gain.imag * now[1]),
            (MIX.real * u[1] + MIX.imag * u[0]) + (gain.real * now[1] + gain.imag * now[0]),
        )
        new = (
            c * now[0] + (u[0] - past[0] - swing * now[1]),
            c * now[1] + (u[1] - past[1] + swing * now[0]),
        )
        past, now = now, new


def carry(span, v0, v1):
    t00, t10, t01, t11, s0, s1 = span
    a, b = sub(v0, s1), add(v1, s0)
    return add(mul(t00, a), mul(t01, b)), add(mul(t10, a), mul(t11, b))


def open_kernel(field, start, end, own, snap, *rest):
    packs, (source, curve, field_in, start_in, end_in, sems) = rest[:4], rest[4:]
    base, slope, swing, _ = constants(DEPTH_STIFFNESS)
    xbase, xslope, _, _ = constants(CROSS_STIFFNESS)
    loads = [
        pltpu.make_async_copy(a, b, sems.at[i])
        for i, (a, b) in enumerate(((field, field_in), (start, start_in), (end, end_in)))
    ]
    for load in loads:
        load.start()
    tiles = field.shape[2] // LANE
    x = lax.axis_index("xr")
    zero = jnp.zeros((CELLS, LANE), jnp.float32)
    for t in range(tiles, SUB):
        spread = pl.ds(t, CELLS, stride=SUB)
        source[0, spread, :] = zero
        source[1, spread, :] = zero
        curve[0, spread, :] = zero + (base + 0.9 * slope)
        curve[1, spread, :] = zero + (xbase + 0.9 * xslope)
    loads[1].wait()
    for t in range(tiles):
        spread, cols = pl.ds(t, CELLS, stride=SUB), slice(t * LANE, (t + 1) * LANE)
        curve[0, spread, :] = base + slope * start_in[:, cols]
    loads[0].wait()
    for t in range(tiles):
        spread, cols = pl.ds(t, CELLS, stride=SUB), slice(t * LANE, (t + 1) * LANE)
        source[0, spread, :] = field_in[0, :, cols]
        source[1, spread, :] = field_in[1, :, cols]
    spans = march_span(source, curve.at[0], swing, CELLS // 4)
    write(own, spans[3])
    for i in range(3):
        write(snap.at[i], spans[i])
    loads[2].wait()
    for t in range(tiles):
        spread, cols = pl.ds(t, CELLS, stride=SUB), slice(t * LANE, (t + 1) * LANE)
        curve[1, spread, :] = xbase + xslope * end_in[:, cols]
    piece = SUB * CELLS // 4
    for d, pack in enumerate(packs):
        first = pl.multiple_of((x ^ d) * piece, piece)
        pack[0:2] = source[:, pl.ds(first, piece), :]
        pack[2:4] = curve[:, pl.ds(first, piece), :]


def turn_kernel(pack, turned):
    turned[...] = pack[3].T


def pair_kernel(axis, bit, own, other, total):
    upper = ((lax.axis_index(axis) >> bit) & 1) == 1
    a, b = read(own), read(other)
    write(total, compose(pick(upper, b, a), pick(upper, a, b)))


def quad_kernel(axis, own, other1, other2, other3, total):
    place = lax.axis_index(axis)
    odd = (place & 1) == 1
    high = (place & 2) == 2
    a, r1, r2, r3 = read(own), read(other1), read(other2), read(other3)
    mine = compose(pick(odd, r1, a), pick(odd, a, r1))
    theirs = compose(pick(odd, r3, r2), pick(odd, r2, r3))
    write(total, compose(pick(high, theirs, mine), pick(high, mine, theirs)))


def descend_pair(left, right, upper, other):
    return (
        pick(upper, normal(advance(left, other)), left),
        pick(upper, right, normal(retreat(right, other))),
    )


def descend_quad(left, right, place, r1, r2, r3):
    odd = (place & 1) == 1
    high = (place & 2) == 2
    first, second = pick(odd, r3, r2), pick(odd, r2, r3)
    left = pick(high, normal(advance(normal(advance(left, first)), second)), left)
    right = pick(high, right, normal(retreat(normal(retreat(right, second)), first)))
    return descend_pair(left, right, odd, r1)


def close_kernel(own, snap, c1, z1, z2, z3, z4, y1, y2, y3, bound0, bound1, bound2, bound3, bounds):
    x, y, z, c = (lax.axis_index(name) for name in ("xr",) + DEPTH)
    left, right = ends(own[0])
    left, right = descend_quad(left, right, y, read(y1), read(y2), read(y3))
    left, right = descend_pair(left, right, (z & 4) == 4, read(z4))
    left, right = descend_quad(left, right, z & 3, read(z1), read(z2), read(z3))
    left, right = descend_pair(left, right, c == 1, read(c1))
    right = normal(retreat(right, read(own)))
    v0, v1 = meet(left, right)
    for i in range(4):
        a, b = carry(read(snap.at[i - 1]), v0, v1) if i else (v0, v1)
        for j, part in enumerate((a[0], a[1], b[0], b[1])):
            bounds[i, j] = part
    for d, bound in enumerate((bound0, bound1, bound2, bound3)):
        bound[...] = bounds[x ^ d]


def cross_kernel(*refs):
    bounds, packs, turns, (result, mid, turned, source, curve, out, sems) = (
        refs[:4], refs[4:8], refs[8:11], refs[11:],
    )
    _, _, swing, gain = constants(DEPTH_STIFFNESS)
    tiles = result.shape[2] // LANE // 4
    x = lax.axis_index("xr")
    lines = CELLS // 4
    for d in range(4):
        pack, bound = packs[d], bounds[d]

        def put(k, re, im, d=d):
            mid[d, 0, rows(k), :] = re
            mid[d, 1, rows(k), :] = im

        march_solution(
            lambda k: (pack[0, rows(k), :], pack[1, rows(k), :]), lambda k: pack[2, rows(k), :],
            swing, gain, (bound[0], bound[1]), (bound[2], bound[3]), put, lines,
        )
    for d in range(4):
        at = x ^ d
        turned[at, 0] = mid[d, 0].T
        turned[at, 1] = mid[d, 1].T
        turned[at, 2] = turns[d][...] if d < 3 else packs[d][3].T
    _, _, swing, gain = constants(CROSS_STIFFNESS)
    for q in range(4):
        for h in range(2):
            spread = pl.ds(2 * q + h, CELLS, stride=SUB)
            half = slice(CELLS * h, CELLS * (h + 1))
            source[0, spread, :] = turned[q, 0, half, :]
            source[1, spread, :] = turned[q, 1, half, :]
            curve[spread, :] = turned[q, 2, half, :]
    (span,) = march_span(source, curve, swing)
    lane = lax.broadcasted_iota(jnp.int32, (SUB, LANE), 1)
    row = lax.broadcasted_iota(jnp.int32, (SUB, LANE), 0)
    zero = jnp.zeros((SUB, LANE), jnp.float32)
    one = zero + 1.0
    unit = [(one, zero), (zero, zero), (zero, zero), (one, zero), (zero, zero), (zero, zero)]
    span = pick((lane & 7) >= tiles, unit, span)
    levels = []
    total = span
    for axis, step in ((0, 1), (1, 1), (1, 2), (1, 4), (0, 2), (0, 4)):
        size = SUB if axis == 0 else LANE
        upper = ((row if axis == 0 else lane) & step) == step

        def swapped(v, axis=axis, step=step, size=size, upper=upper):
            down = pltpu.roll(v, step, axis)
            if 2 * step == size:
                return down
            return jnp.where(upper, down, pltpu.roll(v, size - step, axis))

        other = [(swapped(p[0]), swapped(p[1])) for p in total]
        levels.append((upper, other))
        if len(levels) < 6:
            total = compose(pick(upper, other, total), pick(upper, total, other))
    left, right = ends(zero)
    for upper, other in reversed(levels):
        left, right = descend_pair(left, right, upper, other)
    right = normal(retreat(right, span))
    v0, v1 = meet(left, right)

    def put(k, re, im):
        source[0, rows(k), :] = re
        source[1, rows(k), :] = im

    march_solution(
        lambda k: (source[0, rows(k), :], source[1, rows(k), :]), lambda k: curve[rows(k), :],
        swing, gain, v0, v1, put,
    )
    stores = []
    for part in range(2):
        for q in range(4):
            halves = [source[part, pl.ds(2 * q + h, CELLS, stride=SUB), :] for h in range(2)]
            turned[q, part] = jnp.concatenate(halves, axis=0).T
            for t in range(tiles):
                cols = slice((q * tiles + t) * LANE, (q * tiles + t + 1) * LANE)
                out[part, :, cols] = turned[q, part, pl.ds(t, lines, stride=SUB), :]
            whole = pl.ds(q * tiles * LANE, tiles * LANE)
            store = pltpu.make_async_copy(
                out.at[part, :, whole], result.at[part, :, whole], sems.at[4 * part + q]
            )
            store.start()
            stores.append(store)
    for store in stores:
        store.wait()


def shaped(*shape):
    return jax.ShapeDtypeStruct(shape, jnp.float32)


def call(kernel, outs, scratch=(), far_in=False, far_out=False):
    far, here = pl.BlockSpec(memory_space=pltpu.HBM), pl.BlockSpec(memory_space=pltpu.VMEM)
    out_specs = [far if far_out else here] * len(outs) if isinstance(outs, list) else (far if far_out else here)

    def run(*values):
        return pl.pallas_call(
            kernel,
            out_shape=outs,
            in_specs=[far if far_in else here] * len(values),
            out_specs=out_specs,
            scratch_shapes=list(scratch),
            compiler_params=pltpu.CompilerParams(vmem_limit_bytes=8 << 20),
            cost_estimate=pl.CostEstimate(flops=100000, bytes_accessed=1000000, transcendentals=0),
        )(*values)

    return run


def local(sound_field, index_start, index_end):
    span_shape = shaped(PARTS, SUB, LANE)
    cells = SUB * CELLS
    piece = cells // 4
    inputs = (sound_field, index_start, index_end)
    own, snap, *packs = call(
        open_kernel,
        [span_shape, shaped(3, PARTS, SUB, LANE)] + [shaped(4, piece, LANE)] * 4,
        [pltpu.VMEM((2, cells, LANE), jnp.float32)] * 2
        + [pltpu.VMEM(v.shape, jnp.float32) for v in inputs]
        + [pltpu.SemaphoreType.DMA((3,))],
        far_in=True,
    )(*(pltpu.with_memory_space_constraint(v, pltpu.HBM) for v in inputs))

    def flip(value, axis, d):
        return lax.ppermute(value, axis, [(i, i ^ d) for i in range(lax.axis_size(axis))])

    def pair(axis, bit, a, b):
        return call(lambda *refs: pair_kernel(axis, bit, *refs), span_shape)(a, b)

    def quad(axis, a, others):
        return call(lambda *refs: quad_kernel(axis, *refs), span_shape)(a, *others)

    c1 = flip(own, "c", 1)
    total = pair("c", 0, own, c1)
    zs = [flip(total, "z", d) for d in (1, 2, 3)]
    total = quad("z", total, zs)
    z4 = lax.ppermute(total, "z", [(i, 7 - i) for i in range(8)])
    total = pair("z", 2, total, z4)
    ys = [flip(total, "y", d) for d in (1, 2, 3)]
    bounds = call(
        close_kernel, [shaped(4, SUB, LANE)] * 4, [pltpu.VMEM((4, 4, SUB, LANE), jnp.float32)]
    )(own, snap, c1, *zs, z4, *ys)
    packs = [packs[0]] + [flip(packs[d], "xr", d) for d in (1, 2, 3)]
    turns = []
    for d in TURNS:
        turns.append(call(turn_kernel, shaped(LANE, LANE))(packs[d]))
    bounds = [bounds[0]] + [flip(bounds[d], "xr", d) for d in (1, 2, 3)]
    result = shaped(2, CELLS // 4, 4 * sound_field.shape[2])
    return call(
        cross_kernel,
        result,
        [
            pltpu.VMEM((4, 2, piece, LANE), jnp.float32),
            pltpu.VMEM((4, 3, LANE, LANE), jnp.float32),
            pltpu.VMEM((2, cells, LANE), jnp.float32),
            pltpu.VMEM((cells, LANE), jnp.float32),
            pltpu.VMEM(result.shape, jnp.float32),
            pltpu.SemaphoreType.DMA((8,)),
        ],
        far_out=True,
    )(*bounds, *packs, *turns)


TURNS = (0, 1, 2)


def solution(mesh):
    split = Mesh(mesh.devices.reshape(4, 8, 2, mesh.shape["xr"]), DEPTH + ("xr",))
    in_specs = (P(None, DEPTH, "xr"), P(DEPTH, "xr"), P(DEPTH, "xr"))
    out_specs = P(None, DEPTH + ("xr",), None)

    return jax.shard_map(local, mesh=split, in_specs=in_specs, out_specs=out_specs, check_vma=False)
```

profile of v0, /device:TPU:32, one launch (start us, length us, event | category | flops | bytes accessed | tf_op | source)
XLA Modules:
  0.0 43.9 jit_solution(64607884204065446)
XLA Ops:
  0.0 1.7 %shard_map.37 = (f32[12,8,128]{2,1,0:T(8,128)S(1)}, f32[3,12,8,128]{3,2,1,0:T(8,128)S(1)}, f32[4,128,128]{2,1,0:T(8,128)S(1)}, f32[4,128,128]{2,1,0:T(8,128)S(1)...) custom-call(f32[2,64,896]{2,1,0:T(8,128)} %field.1, f32[64,896]{1,0:T(8,128)} %start.1, f32[64,896]{1,0:T(8,128)} %end.1), custom_call_target="tpu_custom_call" | custom-call | flops 100000 | bytes 1000000 | tf_op jit(solution)/shard_map/pallas_call | solution.py:357
  1.7 0.1 collective-permute-start
  1.8 1.6 %collective-permute-start.11 = (f32[4,128,128]{2,1,0:T(8,128)S(1)}, f32[4,128,128]{2,1,0:T(8,128)S(1)}, u32[]{:S(2)}, u32[]{:S(2)}) collective-permute-start(f32[4,128,128]{2,1,0:T(8,128)S(1)} %get-tuple-element.22), channel_id=1, source_target_pairs={{0,1},{1,0},{2,3},{3,2},{4,5},{5,4},{6,7},{7,6},{8,9},{9,8},{10,11... | collective-permute-start | bytes 786440 | tf_op jit(solution)/shard_map/ppermute | solution.py:385
  3.4 0.0 collective-permute-done.refs_1_.c1
  3.4 2.0 %collective-permute-start.3 = (f32[12,8,128]{2,1,0:T(8,128)S(1)}, f32[12,8,128]{2,1,0:T(8,128)S(1)}, u32[]{:S(2)}, u32[]{:S(2)}) collective-permute-start(f32[12,8,128]{2,1,0:T(8,128)S(1)} %shard_map.38.refs_0_), channel_id=1, source_target_pairs={{0,24},{8,16},{16,8},{24,0},{32,56},{40,48},{48,40},{56,32},{1,25}... | collective-permute-start | bytes 147464 | tf_op jit(solution)/shard_map/ppermute | solution.py:385
  5.5 2.7 %collective-permute-start.12 = (f32[4,128,128]{2,1,0:T(8,128)S(1)}, f32[4,128,128]{2,1,0:T(8,128)S(1)}, u32[]{:S(2)}, u32[]{:S(2)}) collective-permute-start(f32[4,128,128]{2,1,0:T(8,128)S(1)} %get-tuple-element.23), channel_id=1, source_target_pairs={{0,2},{1,3},{2,0},{3,1},{4,6},{5,7},{6,4},{7,5},{8,10},{9,11},{10,... | collective-permute-start | bytes 786440 | tf_op jit(solution)/shard_map/ppermute | solution.py:385
  8.2 1.1 %collective-permute-start.13 = (f32[4,128,128]{2,1,0:T(8,128)S(1)}, f32[4,128,128]{2,1,0:T(8,128)S(1)}, u32[]{:S(2)}, u32[]{:S(2)}) collective-permute-start(f32[4,128,128]{2,1,0:T(8,128)S(1)} %get-tuple-element.24), channel_id=1, source_target_pairs={{0,3},{1,2},{2,1},{3,0},{4,7},{5,6},{6,5},{7,4},{8,11},{9,10},{10,... | collective-permute-start | bytes 786440 | tf_op jit(solution)/shard_map/ppermute | solution.py:385
  9.3 1.7 %collective-permute-start.2 = (f32[12,8,128]{2,1,0:T(8,128)S(1)}, f32[12,8,128]{2,1,0:T(8,128)S(1)}, u32[]{:S(2)}, u32[]{:S(2)}) collective-permute-start(f32[12,8,128]{2,1,0:T(8,128)S(1)} %shard_map.38.refs_0_), channel_id=1, source_target_pairs={{0,16},{8,24},{16,0},{24,8},{32,48},{40,56},{48,32},{56,40},{1,17}... | collective-permute-start | bytes 147464 | tf_op jit(solution)/shard_map/ppermute | solution.py:385
  10.9 0.0 collective-permute-done.3.refs_3_.z3
  10.9 1.1 %collective-permute-start.1 = (f32[12,8,128]{2,1,0:T(8,128)S(1)}, f32[12,8,128]{2,1,0:T(8,128)S(1)}, u32[]{:S(2)}, u32[]{:S(2)}) collective-permute-start(f32[12,8,128]{2,1,0:T(8,128)S(1)} %shard_map.38.refs_0_), channel_id=1, source_target_pairs={{0,8},{8,0},{16,24},{24,16},{32,40},{40,32},{48,56},{56,48},{1,9},... | collective-permute-start | bytes 147464 | tf_op jit(solution)/shard_map/ppermute | solution.py:385
  12.1 2.3 %collective-permute-done.2.refs_2_.z2 = f32[12,8,128]{2,1,0:T(8,128)S(1)} collective-permute-done((f32[12,8,128]{2,1,0:T(8,128)S(1)}, f32[12,8,128]{2,1,0:T(8,128)S(1)}, u32[]{:S(2)}, u32[]{:S(2)}) %collective-permute-start.2) | collective-permute-done | bytes 49184 | tf_op jit(solution)/shard_map/ppermute | solution.py:385
  14.3 0.7 %collective-permute-done.1.refs_1_.z1 = f32[12,8,128]{2,1,0:T(8,128)S(1)} collective-permute-done((f32[12,8,128]{2,1,0:T(8,128)S(1)}, f32[12,8,128]{2,1,0:T(8,128)S(1)}, u32[]{:S(2)}, u32[]{:S(2)}) %collective-permute-start.1) | collective-permute-done | bytes 49184 | tf_op jit(solution)/shard_map/ppermute | solution.py:385
  15.0 0.1 shard_map.39.refs_0_
  15.1 5.7 %collective-permute-start.4 = (f32[12,8,128]{2,1,0:T(8,128)S(1)}, f32[12,8,128]{2,1,0:T(8,128)S(1)}, u32[]{:S(2)}, u32[]{:S(2)}) collective-permute-start(f32[12,8,128]{2,1,0:T(8,128)S(1)} %shard_map.39.refs_0_), channel_id=1, source_target_pairs={{0,56},{8,48},{16,40},{24,32},{32,24},{40,16},{48,8},{56,0},{1,57}... | collective-permute-start | bytes 147464 | tf_op jit(solution)/shard_map/ppermute | solution.py:397
  20.8 2.1 %collective-permute-done.4.refs_1_.z4 = f32[12,8,128]{2,1,0:T(8,128)S(1)} collective-permute-done((f32[12,8,128]{2,1,0:T(8,128)S(1)}, f32[12,8,128]{2,1,0:T(8,128)S(1)}, u32[]{:S(2)}, u32[]{:S(2)}) %collective-permute-start.4) | collective-permute-done | bytes 49184 | tf_op jit(solution)/shard_map/ppermute | solution.py:397
  22.9 3.1 %collective-permute-start.7 = (f32[12,8,128]{2,1,0:T(8,128)S(1)}, f32[12,8,128]{2,1,0:T(8,128)S(1)}, u32[]{:S(2)}, u32[]{:S(2)}) collective-permute-start(f32[12,8,128]{2,1,0:T(8,128)S(1)} %shard_map.40), channel_id=1, source_target_pairs={{0,192},{64,128},{128,64},{192,0},{1,193},{65,129},{129,65},{193,1... | collective-permute-start | bytes 147464 | tf_op jit(solution)/shard_map/ppermute | solution.py:385
  26.0 0.6 %collective-permute-start.6 = (f32[12,8,128]{2,1,0:T(8,128)S(1)}, f32[12,8,128]{2,1,0:T(8,128)S(1)}, u32[]{:S(2)}, u32[]{:S(2)}) collective-permute-start(f32[12,8,128]{2,1,0:T(8,128)S(1)} %shard_map.40), channel_id=1, source_target_pairs={{0,128},{64,192},{128,0},{192,64},{1,129},{65,193},{129,1},{193,65... | collective-permute-start | bytes 147464 | tf_op jit(solution)/shard_map/ppermute | solution.py:385
  26.6 2.1 %collective-permute-done.7.y3 = f32[12,8,128]{2,1,0:T(8,128)S(1)} collective-permute-done((f32[12,8,128]{2,1,0:T(8,128)S(1)}, f32[12,8,128]{2,1,0:T(8,128)S(1)}, u32[]{:S(2)}, u32[]{:S(2)}) %collective-permute-start.7) | collective-permute-done | bytes 49184 | tf_op jit(solution)/shard_map/ppermute | solution.py:385
  28.7 0.1 collective-permute-start.5
  28.8 2.8 %collective-permute-done.6.y2 = f32[12,8,128]{2,1,0:T(8,128)S(1)} collective-permute-done((f32[12,8,128]{2,1,0:T(8,128)S(1)}, f32[12,8,128]{2,1,0:T(8,128)S(1)}, u32[]{:S(2)}, u32[]{:S(2)}) %collective-permute-start.6) | collective-permute-done | bytes 49184 | tf_op jit(solution)/shard_map/ppermute | solution.py:385
  31.6 1.2 %collective-permute-done.5.y1 = f32[12,8,128]{2,1,0:T(8,128)S(1)} collective-permute-done((f32[12,8,128]{2,1,0:T(8,128)S(1)}, f32[12,8,128]{2,1,0:T(8,128)S(1)}, u32[]{:S(2)}, u32[]{:S(2)}) %collective-permute-start.5) | collective-permute-done | bytes 49184 | tf_op jit(solution)/shard_map/ppermute | solution.py:385
  32.8 0.2 shard_map.41
  33.0 0.1 collective-permute-start.8
  33.1 3.6 %collective-permute-start.9 = (f32[4,8,128]{2,1,0:T(8,128)S(1)}, f32[4,8,128]{2,1,0:T(8,128)S(1)}, u32[]{:S(2)}, u32[]{:S(2)}) collective-permute-start(f32[4,8,128]{2,1,0:T(8,128)S(1)} %get-tuple-element.19), channel_id=1, source_target_pairs={{0,2},{1,3},{2,0},{3,1},{4,6},{5,7},{6,4},{7,5},{8,10},{9,11},{10,... | collective-permute-start | bytes 49160 | tf_op jit(solution)/shard_map/ppermute | solution.py:385
  36.6 1.1 %collective-permute-start.10 = (f32[4,8,128]{2,1,0:T(8,128)S(1)}, f32[4,8,128]{2,1,0:T(8,128)S(1)}, u32[]{:S(2)}, u32[]{:S(2)}) collective-permute-start(f32[4,8,128]{2,1,0:T(8,128)S(1)} %get-tuple-element.20), channel_id=1, source_target_pairs={{0,3},{1,2},{2,1},{3,0},{4,7},{5,6},{6,5},{7,4},{8,11},{9,10},{10,... | collective-permute-start | bytes 49160 | tf_op jit(solution)/shard_map/ppermute | solution.py:385
  37.8 0.1 shard_map.42.refs_8_
  37.9 0.1 shard_map.43.refs_9_
  38.0 0.1 shard_map.44.refs_10_
  38.1 0.4 %collective-permute-done.9.refs_2_ = f32[4,8,128]{2,1,0:T(8,128)S(1)} collective-permute-done((f32[4,8,128]{2,1,0:T(8,128)S(1)}, f32[4,8,128]{2,1,0:T(8,128)S(1)}, u32[]{:S(2)}, u32[]{:S(2)}) %collective-permute-start.9) | collective-permute-done | bytes 16416 | tf_op jit(solution)/shard_map/ppermute | solution.py:385
  38.5 3.1 %collective-permute-done.10.refs_3_ = f32[4,8,128]{2,1,0:T(8,128)S(1)} collective-permute-done((f32[4,8,128]{2,1,0:T(8,128)S(1)}, f32[4,8,128]{2,1,0:T(8,128)S(1)}, u32[]{:S(2)}, u32[]{:S(2)}) %collective-permute-start.10) | collective-permute-done | bytes 16416 | tf_op jit(solution)/shard_map/ppermute | solution.py:385
  41.6 0.0 collective-permute-done.13.refs_7_
  41.6 2.3 %shard_map.45 = f32[2,16,3584]{2,1,0:T(8,128)} custom-call(f32[4,8,128]{2,1,0:T(8,128)S(1)} %get-tuple-element.17.refs_0_, f32[4,8,128]{2,1,0:T(8,128)S(1)} %collective-permute-done.8.refs_1_, f32[4,8,128]{2,1,0:T(8,128)S(1)} %collective-permute-done.9.refs_2_, f32[4,8,128]{2,1,0:T(8,128)S(1)} %collective-permute-done.10.refs_3_, ...), custom_call_target="tpu_custom_call" | custom-call | flops 100000 | bytes 1000000 | tf_op jit(solution)/shard_map/pallas_call | solution.py:357
  (5 shorter events, 0.1 us)
Async XLA Ops:
  1.7 1.7 %collective-permute-start = (f32[12,8,128]{2,1,0:T(8,128)S(1)}, f32[12,8,128]{2,1,0:T(8,128)S(1)}, u32[]{:S(2)}, u32[]{:S(2)}) collective-permute-start(f32[12,8,128]{2,1,0:T(8,128)S(1)} %get-tuple-element.15.refs_0_.own), channel_id=1, source_target_pairs={{0,4},{4,0},{1,5},{5,1},{2,6},{6,2},{3,7},{7,3},{8,12},{12,8},{9,1... | collective-permute-start | bytes 147464 | tf_op jit(solution)/shard_map/ppermute | solution.py:385
  1.8 34.8 %collective-permute-start.11 = (f32[4,128,128]{2,1,0:T(8,128)S(1)}, f32[4,128,128]{2,1,0:T(8,128)S(1)}, u32[]{:S(2)}, u32[]{:S(2)}) collective-permute-start(f32[4,128,128]{2,1,0:T(8,128)S(1)} %get-tuple-element.22), channel_id=1, source_target_pairs={{0,1},{1,0},{2,3},{3,2},{4,5},{5,4},{6,7},{7,6},{8,9},{9,8},{10,11... | collective-permute-start | bytes 786440 | tf_op jit(solution)/shard_map/ppermute | solution.py:385
  3.4 7.5 %collective-permute-start.3 = (f32[12,8,128]{2,1,0:T(8,128)S(1)}, f32[12,8,128]{2,1,0:T(8,128)S(1)}, u32[]{:S(2)}, u32[]{:S(2)}) collective-permute-start(f32[12,8,128]{2,1,0:T(8,128)S(1)} %shard_map.38.refs_0_), channel_id=1, source_target_pairs={{0,24},{8,16},{16,8},{24,0},{32,56},{40,48},{48,40},{56,32},{1,25}... | collective-permute-start | bytes 147464 | tf_op jit(solution)/shard_map/ppermute | solution.py:385
  5.5 32.5 %collective-permute-start.12 = (f32[4,128,128]{2,1,0:T(8,128)S(1)}, f32[4,128,128]{2,1,0:T(8,128)S(1)}, u32[]{:S(2)}, u32[]{:S(2)}) collective-permute-start(f32[4,128,128]{2,1,0:T(8,128)S(1)} %get-tuple-element.23), channel_id=1, source_target_pairs={{0,2},{1,3},{2,0},{3,1},{4,6},{5,7},{6,4},{7,5},{8,10},{9,11},{10,... | collective-permute-start | bytes 786440 | tf_op jit(solution)/shard_map/ppermute | solution.py:385
  8.2 33.4 %collective-permute-start.13 = (f32[4,128,128]{2,1,0:T(8,128)S(1)}, f32[4,128,128]{2,1,0:T(8,128)S(1)}, u32[]{:S(2)}, u32[]{:S(2)}) collective-permute-start(f32[4,128,128]{2,1,0:T(8,128)S(1)} %get-tuple-element.24), channel_id=1, source_target_pairs={{0,3},{1,2},{2,1},{3,0},{4,7},{5,6},{6,5},{7,4},{8,11},{9,10},{10,... | collective-permute-start | bytes 786440 | tf_op jit(solution)/shard_map/ppermute | solution.py:385
  9.3 5.1 %collective-permute-start.2 = (f32[12,8,128]{2,1,0:T(8,128)S(1)}, f32[12,8,128]{2,1,0:T(8,128)S(1)}, u32[]{:S(2)}, u32[]{:S(2)}) collective-permute-start(f32[12,8,128]{2,1,0:T(8,128)S(1)} %shard_map.38.refs_0_), channel_id=1, source_target_pairs={{0,16},{8,24},{16,0},{24,8},{32,48},{40,56},{48,32},{56,40},{1,17}... | collective-permute-start | bytes 147464 | tf_op jit(solution)/shard_map/ppermute | solution.py:385
  10.9 4.1 %collective-permute-start.1 = (f32[12,8,128]{2,1,0:T(8,128)S(1)}, f32[12,8,128]{2,1,0:T(8,128)S(1)}, u32[]{:S(2)}, u32[]{:S(2)}) collective-permute-start(f32[12,8,128]{2,1,0:T(8,128)S(1)} %shard_map.38.refs_0_), channel_id=1, source_target_pairs={{0,8},{8,0},{16,24},{24,16},{32,40},{40,32},{48,56},{56,48},{1,9},... | collective-permute-start | bytes 147464 | tf_op jit(solution)/shard_map/ppermute | solution.py:385
  15.1 7.8 %collective-permute-start.4 = (f32[12,8,128]{2,1,0:T(8,128)S(1)}, f32[12,8,128]{2,1,0:T(8,128)S(1)}, u32[]{:S(2)}, u32[]{:S(2)}) collective-permute-start(f32[12,8,128]{2,1,0:T(8,128)S(1)} %shard_map.39.refs_0_), channel_id=1, source_target_pairs={{0,56},{8,48},{16,40},{24,32},{32,24},{40,16},{48,8},{56,0},{1,57}... | collective-permute-start | bytes 147464 | tf_op jit(solution)/shard_map/ppermute | solution.py:397
  22.9 5.8 %collective-permute-start.7 = (f32[12,8,128]{2,1,0:T(8,128)S(1)}, f32[12,8,128]{2,1,0:T(8,128)S(1)}, u32[]{:S(2)}, u32[]{:S(2)}) collective-permute-start(f32[12,8,128]{2,1,0:T(8,128)S(1)} %shard_map.40), channel_id=1, source_target_pairs={{0,192},{64,128},{128,64},{192,0},{1,193},{65,129},{129,65},{193,1... | collective-permute-start | bytes 147464 | tf_op jit(solution)/shard_map/ppermute | solution.py:385
  26.0 5.6 %collective-permute-start.6 = (f32[12,8,128]{2,1,0:T(8,128)S(1)}, f32[12,8,128]{2,1,0:T(8,128)S(1)}, u32[]{:S(2)}, u32[]{:S(2)}) collective-permute-start(f32[12,8,128]{2,1,0:T(8,128)S(1)} %shard_map.40), channel_id=1, source_target_pairs={{0,128},{64,192},{128,0},{192,64},{1,129},{65,193},{129,1},{193,65... | collective-permute-start | bytes 147464 | tf_op jit(solution)/shard_map/ppermute | solution.py:385
  28.7 4.1 %collective-permute-start.5 = (f32[12,8,128]{2,1,0:T(8,128)S(1)}, f32[12,8,128]{2,1,0:T(8,128)S(1)}, u32[]{:S(2)}, u32[]{:S(2)}) collective-permute-start(f32[12,8,128]{2,1,0:T(8,128)S(1)} %shard_map.40), channel_id=1, source_target_pairs={{0,64},{64,0},{128,192},{192,128},{1,65},{65,1},{129,193},{193,129... | collective-permute-start | bytes 147464 | tf_op jit(solution)/shard_map/ppermute | solution.py:385
  33.0 5.1 %collective-permute-start.8 = (f32[4,8,128]{2,1,0:T(8,128)S(1)}, f32[4,8,128]{2,1,0:T(8,128)S(1)}, u32[]{:S(2)}, u32[]{:S(2)}) collective-permute-start(f32[4,8,128]{2,1,0:T(8,128)S(1)} %get-tuple-element.18), channel_id=1, source_target_pairs={{0,1},{1,0},{2,3},{3,2},{4,5},{5,4},{6,7},{7,6},{8,9},{9,8},{10,11... | collective-permute-start | bytes 49160 | tf_op jit(solution)/shard_map/ppermute | solution.py:385
  33.1 5.4 %collective-permute-start.9 = (f32[4,8,128]{2,1,0:T(8,128)S(1)}, f32[4,8,128]{2,1,0:T(8,128)S(1)}, u32[]{:S(2)}, u32[]{:S(2)}) collective-permute-start(f32[4,8,128]{2,1,0:T(8,128)S(1)} %get-tuple-element.19), channel_id=1, source_target_pairs={{0,2},{1,3},{2,0},{3,1},{4,6},{5,7},{6,4},{7,5},{8,10},{9,11},{10,... | collective-permute-start | bytes 49160 | tf_op jit(solution)/shard_map/ppermute | solution.py:385
  36.6 5.0 %collective-permute-start.10 = (f32[4,8,128]{2,1,0:T(8,128)S(1)}, f32[4,8,128]{2,1,0:T(8,128)S(1)}, u32[]{:S(2)}, u32[]{:S(2)}) collective-permute-start(f32[4,8,128]{2,1,0:T(8,128)S(1)} %get-tuple-element.20), channel_id=1, source_target_pairs={{0,3},{1,2},{2,1},{3,0},{4,7},{5,6},{6,5},{7,4},{8,11},{9,10},{10,... | collective-permute-start | bytes 49160 | tf_op jit(solution)/shard_map/ppermute | solution.py:385
where the time goes:
time: 44 us; the launch traced here: 43.9 us
  starting transfers between devices  24.7 us (56%)
  waiting for transfers between devices  14.6 us (33%)
  Pallas kernels  4.6 us (10%)
    ppermute x13, starting transfers between devices, flip(): lax.ppermute(value, axis, [(i, i ^ d) for i in range(lax.axis_size(axis))])  18.9 us
    ppermute x13, waiting for transfers between devices, flip(): lax.ppermute(value, axis, [(i, i ^ d) for i in range(lax.axis_size(axis))])  12.5 us
    ppermute x1, starting transfers between devices, local(): z4 = lax.ppermute(total, 'z', [(i, 7 - i) for i in range(8)])  5.73 us
    pallas_call x9, Pallas kernels, run(): pl.pallas_call(kernel, out_shape=outs, in_specs=[far if far_in else here]...  4.6 us
    ppermute x1, waiting for transfers between devices, local(): z4 = lax.ppermute(total, 'z', [(i, 7 - i) for i in range(8)])  2.07 us
  transfers between devices with their start and end apart: 14, of which 8 were waited for; matrix products, arithmetic and copies ran while one was open for 0% of the time, Pallas kernels for 1%

commit v1 on v0

--- a/solution.py
+++ b/solution.py
@@ -13,7 +13,7 @@
 NUMER = complex(2.857, 0.004)
 DENOM = complex(2.857, -0.004)
 
-MIX = NUMER / DENOM
+MIX = (NUMER / DENOM) ** 2
 
 SUB = 8
 LANE = 128
@@ -25,8 +25,8 @@
     slope = -0.5 / stiffness
     base = 2.0 - (1.0 / DENOM).real / stiffness - slope
     swing = -(1.0 / DENOM).imag / stiffness
-    gain = (1.0 - MIX) / (stiffness * DENOM)
-    return base, slope, swing, gain
+    push = ((DENOM - NUMER) / (NUMER * DENOM * stiffness)).imag
+    return base, slope, swing, push
 
 
 def mul(a, b):
@@ -120,89 +120,105 @@
     return pl.ds(SUB * k, SUB)
 
 
-def march_span(source, curve, swing, every=CELLS):
+def step(c, swing, now, past, u=None):
+    if u is not None:
+        past = sub(past, u)
+    return (c * now[0] - (swing * now[1] + past[0]), c * now[1] + (swing * now[0] - past[1]))
+
+
+def start_pair():
     zero = jnp.zeros((SUB, LANE), jnp.float32)
     one = zero + 1.0
-    past = [(one, zero), (zero, zero)]
-    now = [(zero, zero), (one, zero)]
-    sums = [(zero, zero), (zero, zero)]
-    spans = []
-    for k in range(CELLS):
-        u = source[0, rows(k), :], source[1, rows(k), :]
-        c = curve[rows(k), :]
-        for i in range(2):
-            p, n = past[i], now[i]
-            sums[i] = add(sums[i], mul(n, u))
-            new = (c * n[0] - (swing * n[1] + p[0]), c * n[1] + (swing * n[0] - p[1]))
-            past[i], now[i] = n, new
-        if (k + 1) % every == 0:
-            spans.append([past[0], now[0], past[1], now[1], sums[0], sums[1]])
-    return spans
-
-
-def march_solution(source, curve, swing, gain, v0, v1, target, count=CELLS):
-    past, now = v0, v1
-    for k in range(count):
-        u, c = source(k), curve(k)
-        target(
-            k,
-            (MIX.real * u[0] - MIX.imag * u[1]) + (gain.real * now[0] - gain.imag * now[1]),
-            (MIX.real * u[1] + MIX.imag * u[0]) + (gain.real * now[1] + gain.imag * now[0]),
-        )
-        new = (
-            c * now[0] + (u[0] - past[0] - swing * now[1]),
-            c * now[1] + (u[1] - past[1] + swing * now[0]),
-        )
-        past, now = now, new
-
-
-def carry(span, v0, v1):
-    t00, t10, t01, t11, s0, s1 = span
-    a, b = sub(v0, s1), add(v1, s0)
-    return add(mul(t00, a), mul(t01, b)), add(mul(t10, a), mul(t11, b))
-
-
-def open_kernel(field, start, end, own, snap, *rest):
-    packs, (source, curve, field_in, start_in, end_in, sems) = rest[:4], rest[4:]
+    return [[(one, zero), (zero, zero)], [(zero, zero), (one, zero)]]
+
+
+def still():
+    zero = jnp.zeros((SUB, LANE), jnp.float32)
+    return [(zero, zero), (zero, zero)]
+
+
+def through(matrix, v0, v1):
+    t00, t10, t01, t11 = matrix
+    return add(mul(t00, v0), mul(t01, v1)), add(mul(t10, v0), mul(t11, v1))
+
+
+def product(late, early):
+    first = through(late, early[0], early[1])
+    second = through(late, early[2], early[3])
+    return [first[0], first[1], second[0], second[1]]
+
+
+def sums_of(matrix, p0, p1):
+    t00, t10, t01, t11 = matrix
+    return sub(mul(t00, p1), mul(t10, p0)), sub(mul(t01, p1), mul(t11, p0))
+
+
+def read_all(ref, first, count):
+    return [(ref[first + 2 * i], ref[first + 2 * i + 1]) for i in range(count)]
+
+
+def write_all(ref, first, parts):
+    for i, part in enumerate(parts):
+        ref[first + 2 * i] = part[0]
+        ref[first + 2 * i + 1] = part[1]
+
+
+def open_kernel(field, start, end, own, snap, source, curve, end_in, field_in, start_in, sems):
     base, slope, swing, _ = constants(DEPTH_STIFFNESS)
-    xbase, xslope, _, _ = constants(CROSS_STIFFNESS)
     loads = [
         pltpu.make_async_copy(a, b, sems.at[i])
-        for i, (a, b) in enumerate(((field, field_in), (start, start_in), (end, end_in)))
+        for i, (a, b) in enumerate(((start, start_in), (field, field_in), (end, end_in)))
     ]
     for load in loads:
         load.start()
     tiles = field.shape[2] // LANE
-    x = lax.axis_index("xr")
     zero = jnp.zeros((CELLS, LANE), jnp.float32)
     for t in range(tiles, SUB):
         spread = pl.ds(t, CELLS, stride=SUB)
         source[0, spread, :] = zero
         source[1, spread, :] = zero
-        curve[0, spread, :] = zero + (base + 0.9 * slope)
-        curve[1, spread, :] = zero + (xbase + 0.9 * xslope)
-    loads[1].wait()
+        curve[spread, :] = zero + (base + 0.9 * slope)
+    loads[0].wait()
     for t in range(tiles):
         spread, cols = pl.ds(t, CELLS, stride=SUB), slice(t * LANE, (t + 1) * LANE)
-        curve[0, spread, :] = base + slope * start_in[:, cols]
-    loads[0].wait()
+        curve[spread, :] = base + slope * start_in[:, cols]
+    loads[1].wait()
     for t in range(tiles):
         spread, cols = pl.ds(t, CELLS, stride=SUB), slice(t * LANE, (t + 1) * LANE)
         source[0, spread, :] = field_in[0, :, cols]
         source[1, spread, :] = field_in[1, :, cols]
-    spans = march_span(source, curve.at[0], swing, CELLS // 4)
-    write(own, spans[3])
-    for i in range(3):
-        write(snap.at[i], spans[i])
+    waves = start_pair()
+    march = still()
+    for k in range(CELLS):
+        u, c = (source[0, rows(k), :], source[1, rows(k), :]), curve[rows(k), :]
+        march = [march[1], step(c, swing, march[1], march[0], u)]
+        waves = [[w[1], step(c, swing, w[1], w[0])] for w in waves]
+        if k % (CELLS // 4) == CELLS // 4 - 1 and k < CELLS - 1:
+            write(snap.at[k // (CELLS // 4)], waves[0] + waves[1] + march)
+    matrix = waves[0] + waves[1]
+    write(own, matrix + list(sums_of(matrix, *march)))
     loads[2].wait()
-    for t in range(tiles):
-        spread, cols = pl.ds(t, CELLS, stride=SUB), slice(t * LANE, (t + 1) * LANE)
-        curve[1, spread, :] = xbase + xslope * end_in[:, cols]
-    piece = SUB * CELLS // 4
+
+
+def stow_kernel(source, curve, end, *packs):
+    xbase, xslope, _, _ = constants(CROSS_STIFFNESS)
+    tiles = end.shape[1] // LANE
+    x = lax.axis_index("xr")
+    count = CELLS // 4
     for d, pack in enumerate(packs):
-        first = pl.multiple_of((x ^ d) * piece, piece)
-        pack[0:2] = source[:, pl.ds(first, piece), :]
-        pack[2:4] = curve[:, pl.ds(first, piece), :]
+        here = pl.ds(pl.multiple_of((x ^ d) * SUB * count, SUB * count), SUB * count)
+        re, im = source[0, here, :], source[1, here, :]
+        pack[0] = MIX.real * re - MIX.imag * im
+        pack[1] = MIX.real * im + MIX.imag * re
+        pack[2] = curve[here, :]
+        first = pl.multiple_of((x ^ d) * count, count)
+        for t in range(tiles):
+            cols = slice(t * LANE, (t + 1) * LANE)
+            pack[3, pl.ds(t, count, stride=SUB), :] = xbase + xslope * end[pl.ds(first, count), cols]
+        for t in range(tiles, SUB):
+            pack[3, pl.ds(t, count, stride=SUB), :] = jnp.zeros((count, LANE), jnp.float32) + (
+                xbase + 0.9 * xslope
+            )
 
 
 def turn_kernel(pack, turned):
@@ -251,85 +267,178 @@
     right = normal(retreat(right, read(own)))
     v0, v1 = meet(left, right)
     for i in range(4):
-        a, b = carry(read(snap.at[i - 1]), v0, v1) if i else (v0, v1)
-        for j, part in enumerate((a[0], a[1], b[0], b[1])):
-            bounds[i, j] = part
+        a, b = v0, v1
+        if i:
+            span = read(snap.at[i - 1])
+            a, b = through(span[:4], v0, v1)
+            a, b = add(a, span[4]), add(b, span[5])
+        for j, part in enumerate((a, b)):
+            bounds[i, 2 * j] = MIX.real * part[0] - MIX.imag * part[1]
+            bounds[i, 2 * j + 1] = MIX.real * part[1] + MIX.imag * part[0]
     for d, bound in enumerate((bound0, bound1, bound2, bound3)):
         bound[...] = bounds[x ^ d]
 
 
+LEVELS = ((0, 1), (1, 1), (1, 2), (1, 4), (0, 2), (0, 4))
+HALF = CELLS // 2
+LATE, WHOLE, SOLVE, OWN, LEVEL0, PER_LEVEL = 8, 16, 24, 32, 36, 16
+
+
+def upper_of(axis, stride):
+    return (lax.broadcasted_iota(jnp.int32, (SUB, LANE), axis) & stride) == stride
+
+
+def swapped(v, axis, stride, upper):
+    size = SUB if axis == 0 else LANE
+    down = pltpu.roll(v, stride, axis)
+    if 2 * stride == size:
+        return down
+    return jnp.where(upper, down, pltpu.roll(v, size - stride, axis))
+
+
+def swapped_all(parts, axis, stride, upper):
+    return [(swapped(p[0], axis, stride, upper), swapped(p[1], axis, stride, upper)) for p in parts]
+
+
+def plan_kernel(*refs):
+    tiles, turns, last, curve, plan, whole = refs[0], refs[1:4], refs[4], refs[5], refs[6], refs[7]
+    _, _, swing, _ = constants(CROSS_STIFFNESS)
+    x = lax.axis_index("xr")
+    for d in range(4):
+        whole[x ^ d] = turns[d][...] if d < 3 else last[3].T
+    for q in range(4):
+        for h in range(2):
+            curve[pl.ds(2 * q + h, CELLS, stride=SUB), :] = whole[q, CELLS * h : CELLS * (h + 1), :]
+    halves = [start_pair(), start_pair()]
+    for k in range(HALF):
+        for h in range(2):
+            c = curve[rows(k + HALF * h), :]
+            halves[h] = [[w[1], step(c, swing, w[1], w[0])] for w in halves[h]]
+    early, late = (w[0] + w[1] for w in halves)
+    write_all(plan, 0, early)
+    write_all(plan, LATE, late)
+    matrix = product(late, early)
+    write_all(plan, WHOLE, matrix)
+    lane = lax.broadcasted_iota(jnp.int32, (SUB, LANE), 1)
+    unit = start_pair()
+    unit = unit[0] + unit[1]
+    matrix = pick((lane & 7) >= tiles, unit, matrix)
+    total = matrix
+    stages = []
+    for i, (axis, stride) in enumerate(LEVELS):
+        upper = upper_of(axis, stride)
+        other = swapped_all(total, axis, stride, upper)
+        low = pick(upper, other, total)
+        stages.append((upper, other))
+        if i < 5:
+            write_all(plan, LEVEL0 + PER_LEVEL * i, low)
+            total = product(pick(upper, total, other), low)
+    zero = jnp.zeros((SUB, LANE), jnp.float32)
+    one = zero + 1.0
+    left, right = [(zero, zero), (one, zero)], [(one, zero), (zero, zero)]
+    left_weights, right_weights = [], []
+
+    def rescale(pair, weights):
+        size = jnp.maximum(
+            jnp.maximum(jnp.abs(pair[0][0]), jnp.abs(pair[0][1])),
+            jnp.maximum(jnp.abs(pair[1][0]), jnp.abs(pair[1][1])),
+        )
+        scale = 1.0 / size
+        return [scaled(p, scale) for p in pair], [[scaled(w, scale) for w in ws] for ws in weights]
+
+    for upper, other in reversed(stages):
+        gone = list(through(other, left[0], left[1]))
+        left_weights.append([scaled(p, jnp.where(upper, 1.0, 0.0)) for p in left])
+        left, left_weights = rescale(pick(upper, gone, left), left_weights)
+        t00, t10, t01, t11 = other
+        back = [sub(mul(t11, right[0]), mul(t01, right[1])), sub(mul(t00, right[1]), mul(t10, right[0]))]
+        right_weights.append([scaled(p, jnp.where(upper, 0.0, 1.0)) for p in back])
+        right, right_weights = rescale(pick(upper, right, back), right_weights)
+    t00, t10, t01, t11 = matrix
+    right = [sub(mul(t11, right[0]), mul(t01, right[1])), sub(mul(t00, right[1]), mul(t10, right[0]))]
+    right_weights.append(right)
+    right, right_weights = rescale(right, right_weights)
+    det = sub(mul(left[1], right[0]), mul(left[0], right[1]))
+    scale = -1.0 / (det[0] * det[0] + det[1] * det[1])
+    inverse = (det[0] * scale, -det[1] * scale)
+    write_all(plan, SOLVE, [mul(p, inverse) for p in (left[0], right[0], right[1], left[1])])
+    write_all(plan, OWN, right_weights[-1])
+    for i in range(6):
+        write_all(plan, LEVEL0 + PER_LEVEL * i + 8, left_weights[5 - i] + right_weights[5 - i])
+
+
 def cross_kernel(*refs):
-    bounds, packs, turns, (result, mid, turned, source, curve, out, sems) = (
-        refs[:4], refs[4:8], refs[8:11], refs[11:],
+    bounds, packs, curve, plan, (result, mid, turned, source, out, sems) = (
+        refs[:4], refs[4:8], refs[8], refs[9], refs[10:],
     )
-    _, _, swing, gain = constants(DEPTH_STIFFNESS)
+    _, _, swing, push = constants(DEPTH_STIFFNESS)
     tiles = result.shape[2] // LANE // 4
     x = lax.axis_index("xr")
     lines = CELLS // 4
     for d in range(4):
         pack, bound = packs[d], bounds[d]
-
-        def put(k, re, im, d=d):
-            mid[d, 0, rows(k), :] = re
-            mid[d, 1, rows(k), :] = im
-
-        march_solution(
-            lambda k: (pack[0, rows(k), :], pack[1, rows(k), :]), lambda k: pack[2, rows(k), :],
-            swing, gain, (bound[0], bound[1]), (bound[2], bound[3]), put, lines,
-        )
-    for d in range(4):
+        past, now = (bound[0], bound[1]), (bound[2], bound[3])
+        for k in range(lines):
+            u, c = (pack[0, rows(k), :], pack[1, rows(k), :]), pack[2, rows(k), :]
+            mid[d, 0, rows(k), :] = u[0] - push * now[1]
+            mid[d, 1, rows(k), :] = u[1] + push * now[0]
+            past, now = now, step(c, swing, now, past, u)
         at = x ^ d
         turned[at, 0] = mid[d, 0].T
         turned[at, 1] = mid[d, 1].T
-        turned[at, 2] = turns[d][...] if d < 3 else packs[d][3].T
-    _, _, swing, gain = constants(CROSS_STIFFNESS)
+    _, _, swing, push = constants(CROSS_STIFFNESS)
     for q in range(4):
         for h in range(2):
             spread = pl.ds(2 * q + h, CELLS, stride=SUB)
             half = slice(CELLS * h, CELLS * (h + 1))
             source[0, spread, :] = turned[q, 0, half, :]
             source[1, spread, :] = turned[q, 1, half, :]
-            curve[spread, :] = turned[q, 2, half, :]
-    (span,) = march_span(source, curve, swing)
-    lane = lax.broadcasted_iota(jnp.int32, (SUB, LANE), 1)
-    row = lax.broadcasted_iota(jnp.int32, (SUB, LANE), 0)
+
+    def cell(k):
+        return (source[0, rows(k), :], source[1, rows(k), :]), curve[rows(k), :]
+
+    marches = [still(), still()]
+    for k in range(HALF):
+        for h in range(2):
+            u, c = cell(k + HALF * h)
+            past, now = marches[h]
+            marches[h] = [now, step(c, swing, now, past, u)]
+    early, late, matrix = (read_all(plan, first, 4) for first in (0, LATE, WHOLE))
+    end0, end1 = through(late, *marches[0])
+    end0, end1 = add(end0, marches[1][0]), add(end1, marches[1][1])
+    valid = (lax.broadcasted_iota(jnp.int32, (SUB, LANE), 1) & 7) < tiles
     zero = jnp.zeros((SUB, LANE), jnp.float32)
-    one = zero + 1.0
-    unit = [(one, zero), (zero, zero), (zero, zero), (one, zero), (zero, zero), (zero, zero)]
-    span = pick((lane & 7) >= tiles, unit, span)
-    levels = []
-    total = span
-    for axis, step in ((0, 1), (1, 1), (1, 2), (1, 4), (0, 2), (0, 4)):
-        size = SUB if axis == 0 else LANE
-        upper = ((row if axis == 0 else lane) & step) == step
-
-        def swapped(v, axis=axis, step=step, size=size, upper=upper):
-            down = pltpu.roll(v, step, axis)
-            if 2 * step == size:
-                return down
-            return jnp.where(upper, down, pltpu.roll(v, size - step, axis))
-
-        other = [(swapped(p[0]), swapped(p[1])) for p in total]
-        levels.append((upper, other))
-        if len(levels) < 6:
-            total = compose(pick(upper, other, total), pick(upper, total, other))
-    left, right = ends(zero)
-    for upper, other in reversed(levels):
-        left, right = descend_pair(left, right, upper, other)
-    right = normal(retreat(right, span))
-    v0, v1 = meet(left, right)
-
-    def put(k, re, im):
-        source[0, rows(k), :] = re
-        source[1, rows(k), :] = im
-
-    march_solution(
-        lambda k: (source[0, rows(k), :], source[1, rows(k), :]), lambda k: curve[rows(k), :],
-        swing, gain, v0, v1, put,
-    )
+    sums = [(jnp.where(valid, s[0], zero), jnp.where(valid, s[1], zero)) for s in sums_of(matrix, end0, end1)]
+    w0, w1 = read_all(plan, OWN, 2)
+    g, h = (zero, zero), add(mul(w0, sums[0]), mul(w1, sums[1]))
+    for i, (axis, stride) in enumerate(LEVELS):
+        upper = upper_of(axis, stride)
+        other = swapped_all(sums, axis, stride, upper)
+        l0, l1, r0, r1 = read_all(plan, LEVEL0 + PER_LEVEL * i + 8, 4)
+        g = add(g, add(mul(l0, other[0]), mul(l1, other[1])))
+        h = add(h, add(mul(r0, other[0]), mul(r1, other[1])))
+        if i < 5:
+            t00, t10, t01, t11 = read_all(plan, LEVEL0 + PER_LEVEL * i, 4)
+            low, high = pick(upper, other, sums), pick(upper, sums, other)
+            sums = [
+                add(low[0], add(mul(t00, high[0]), mul(t10, high[1]))),
+                add(low[1], add(mul(t01, high[0]), mul(t11, high[1]))),
+            ]
+    f0, p0, p1, f1 = read_all(plan, SOLVE, 4)
+    v0 = add(mul(f0, h), mul(p0, g))
+    v1 = add(mul(p1, g), mul(f1, h))
+    half = through(early, v0, v1)
+    states = [[v0, v1], [add(half[0], marches[0][0]), add(half[1], marches[0][1])]]
+    for k in range(HALF):
+        for h in range(2):
+            u, c = cell(k + HALF * h)
+            past, now = states[h]
+            source[0, rows(k + HALF * h), :] = u[0] - push * now[1]
+            source[1, rows(k + HALF * h), :] = u[1] + push * now[0]
+            states[h] = [now, step(c, swing, now, past, u)]
     stores = []
-    for part in range(2):
-        for q in range(4):
+    for q in range(4):
+        for part in range(2):
             halves = [source[part, pl.ds(2 * q + h, CELLS, stride=SUB), :] for h in range(2)]
             turned[q, part] = jnp.concatenate(halves, axis=0).T
             for t in range(tiles):
@@ -372,14 +481,19 @@
     cells = SUB * CELLS
     piece = cells // 4
     inputs = (sound_field, index_start, index_end)
-    own, snap, *packs = call(
+    own, snap, source, curve, end = call(
         open_kernel,
-        [span_shape, shaped(3, PARTS, SUB, LANE)] + [shaped(4, piece, LANE)] * 4,
-        [pltpu.VMEM((2, cells, LANE), jnp.float32)] * 2
-        + [pltpu.VMEM(v.shape, jnp.float32) for v in inputs]
-        + [pltpu.SemaphoreType.DMA((3,))],
+        [
+            span_shape,
+            shaped(3, PARTS, SUB, LANE),
+            shaped(2, cells, LANE),
+            shaped(cells, LANE),
+            shaped(*index_end.shape),
+        ],
+        [pltpu.VMEM(v.shape, jnp.float32) for v in inputs[:2]] + [pltpu.SemaphoreType.DMA((3,))],
         far_in=True,
     )(*(pltpu.with_memory_space_constraint(v, pltpu.HBM) for v in inputs))
+    packs = call(stow_kernel, [shaped(4, piece, LANE)] * 4)(source, curve, end)
 
     def flip(value, axis, d):
         return lax.ppermute(value, axis, [(i, i ^ d) for i in range(lax.axis_size(axis))])
@@ -405,20 +519,25 @@
     for d in TURNS:
         turns.append(call(turn_kernel, shaped(LANE, LANE))(packs[d]))
     bounds = [bounds[0]] + [flip(bounds[d], "xr", d) for d in (1, 2, 3)]
+    tiles = sound_field.shape[2] // LANE
+    curve, plan = call(
+        lambda *refs: plan_kernel(tiles, *refs),
+        [shaped(cells, LANE), shaped(LEVEL0 + 6 * PER_LEVEL, SUB, LANE)],
+        [pltpu.VMEM((4, LANE, LANE), jnp.float32)],
+    )(*turns, packs[3])
     result = shaped(2, CELLS // 4, 4 * sound_field.shape[2])
     return call(
         cross_kernel,
         result,
         [
             pltpu.VMEM((4, 2, piece, LANE), jnp.float32),
-            pltpu.VMEM((4, 3, LANE, LANE), jnp.float32),
+            pltpu.VMEM((4, 2, LANE, LANE), jnp.float32),
             pltpu.VMEM((2, cells, LANE), jnp.float32),
-            pltpu.VMEM((cells, LANE), jnp.float32),
             pltpu.VMEM(result.shape, jnp.float32),
             pltpu.SemaphoreType.DMA((8,)),
         ],
         far_out=True,
-    )(*bounds, *packs, *turns)
+    )(*bounds, *packs, curve, plan)
 
 
 TURNS = (0, 1, 2)

time: 44 us -> 43.6 us (level)
    pallas_call x9 -> x11, Pallas kernels: 4.6 us -> 4.81 us  [run(): pl.pallas_call(kernel, out_shape=outs, in_specs=[far if far_in else here]...]
  transfers between devices with their start and end apart: 14 -> 14, of which waited for: 8 -> 7; matrix products, arithmetic and copies ran while one was open for 0% -> 0% of each run, Pallas kernels for 1% -> 3%
where the time goes in v1:
time: 43.6 us; the launch traced here: 43.5 us
  starting transfers between devices  24.4 us (56%)
  waiting for transfers between devices  14.2 us (33%)
  Pallas kernels  4.81 us (11%)
    ppermute x13, starting transfers between devices, flip(): lax.ppermute(value, axis, [(i, i ^ d) for i in range(lax.axis_size(axis))])  18.8 us
    ppermute x13, waiting for transfers between devices, flip(): lax.ppermute(value, axis, [(i, i ^ d) for i in range(lax.axis_size(axis))])  12.1 us
    ppermute x1, starting transfers between devices, local(): z4 = lax.ppermute(total, 'z', [(i, 7 - i) for i in range(8)])  5.57 us
    pallas_call x11, Pallas kernels, run(): pl.pallas_call(kernel, out_shape=outs, in_specs=[far if far_in else here]...  4.81 us
    ppermute x1, waiting for transfers between devices, local(): z4 = lax.ppermute(total, 'z', [(i, 7 - i) for i in range(8)])  2.07 us
  transfers between devices with their start and end apart: 14, of which 7 were waited for; matrix products, arithmetic and copies ran while one was open for 0% of the time, Pallas kernels for 3%

profile of v1, /device:TPU:32, one launch (start us, length us, event | category | flops | bytes accessed | tf_op | source)
XLA Modules:
  0.0 43.5 jit_solution(7386461137898355271)
XLA Ops:
  0.0 1.5 %shard_map.37 = (f32[12,8,128]{2,1,0:T(8,128)S(1)}, f32[3,12,8,128]{3,2,1,0:T(8,128)S(1)}, f32[2,512,128]{2,1,0:T(8,128)S(1)}, f32[512,128]{1,0:T(8,128)S(1)}, f32[64,896]{1,0:T(8,128)S(1)}) custom-call(f32[2,64,896]{2,1,0:T(8,128)} %field.1, f32[64,896]{1,0:T(8,128)} %start.1, f32[64,896]{1,0:T(8,128)} %end.1), custom_call_target="tpu_custom_call" | custom-call | flops 100000 | bytes 1000000 | tf_op jit(solution)/shard_map/pallas_call | solution.py:466
  1.5 0.1 collective-permute-start
  1.6 0.1 shard_map.42
  1.8 1.6 %collective-permute-start.11 = (f32[4,128,128]{2,1,0:T(8,128)S(1)}, f32[4,128,128]{2,1,0:T(8,128)S(1)}, u32[]{:S(2)}, u32[]{:S(2)}) collective-permute-start(f32[4,128,128]{2,1,0:T(8,128)S(1)} %get-tuple-element.30), channel_id=1, source_target_pairs={{0,1},{1,0},{2,3},{3,2},{4,5},{5,4},{6,7},{7,6},{8,9},{9,8},{10,11... | collective-permute-start | bytes 786440 | tf_op jit(solution)/shard_map/ppermute | solution.py:499
  3.4 0.0 collective-permute-done.refs_1_.c1
  3.4 2.0 %collective-permute-start.3 = (f32[12,8,128]{2,1,0:T(8,128)S(1)}, f32[12,8,128]{2,1,0:T(8,128)S(1)}, u32[]{:S(2)}, u32[]{:S(2)}) collective-permute-start(f32[12,8,128]{2,1,0:T(8,128)S(1)} %shard_map.38.refs_0_), channel_id=1, source_target_pairs={{0,24},{8,16},{16,8},{24,0},{32,56},{40,48},{48,40},{56,32},{1,25}... | collective-permute-start | bytes 147464 | tf_op jit(solution)/shard_map/ppermute | solution.py:499
  5.4 2.7 %collective-permute-start.12 = (f32[4,128,128]{2,1,0:T(8,128)S(1)}, f32[4,128,128]{2,1,0:T(8,128)S(1)}, u32[]{:S(2)}, u32[]{:S(2)}) collective-permute-start(f32[4,128,128]{2,1,0:T(8,128)S(1)} %get-tuple-element.31), channel_id=1, source_target_pairs={{0,2},{1,3},{2,0},{3,1},{4,6},{5,7},{6,4},{7,5},{8,10},{9,11},{10,... | collective-permute-start | bytes 786440 | tf_op jit(solution)/shard_map/ppermute | solution.py:499
  8.1 0.9 %collective-permute-start.13 = (f32[4,128,128]{2,1,0:T(8,128)S(1)}, f32[4,128,128]{2,1,0:T(8,128)S(1)}, u32[]{:S(2)}, u32[]{:S(2)}) collective-permute-start(f32[4,128,128]{2,1,0:T(8,128)S(1)} %get-tuple-element.32), channel_id=1, source_target_pairs={{0,3},{1,2},{2,1},{3,0},{4,7},{5,6},{6,5},{7,4},{8,11},{9,10},{10,... | collective-permute-start | bytes 786440 | tf_op jit(solution)/shard_map/ppermute | solution.py:499
  9.1 1.8 %collective-permute-start.2 = (f32[12,8,128]{2,1,0:T(8,128)S(1)}, f32[12,8,128]{2,1,0:T(8,128)S(1)}, u32[]{:S(2)}, u32[]{:S(2)}) collective-permute-start(f32[12,8,128]{2,1,0:T(8,128)S(1)} %shard_map.38.refs_0_), channel_id=1, source_target_pairs={{0,16},{8,24},{16,0},{24,8},{32,48},{40,56},{48,32},{56,40},{1,17}... | collective-permute-start | bytes 147464 | tf_op jit(solution)/shard_map/ppermute | solution.py:499
  10.9 0.0 collective-permute-done.3.refs_3_.z3
  10.9 1.0 %collective-permute-start.1 = (f32[12,8,128]{2,1,0:T(8,128)S(1)}, f32[12,8,128]{2,1,0:T(8,128)S(1)}, u32[]{:S(2)}, u32[]{:S(2)}) collective-permute-start(f32[12,8,128]{2,1,0:T(8,128)S(1)} %shard_map.38.refs_0_), channel_id=1, source_target_pairs={{0,8},{8,0},{16,24},{24,16},{32,40},{40,32},{48,56},{56,48},{1,9},... | collective-permute-start | bytes 147464 | tf_op jit(solution)/shard_map/ppermute | solution.py:499
  11.9 2.3 %collective-permute-done.2.refs_2_.z2 = f32[12,8,128]{2,1,0:T(8,128)S(1)} collective-permute-done((f32[12,8,128]{2,1,0:T(8,128)S(1)}, f32[12,8,128]{2,1,0:T(8,128)S(1)}, u32[]{:S(2)}, u32[]{:S(2)}) %collective-permute-start.2) | collective-permute-done | bytes 49184 | tf_op jit(solution)/shard_map/ppermute | solution.py:499
  14.1 0.8 %collective-permute-done.1.refs_1_.z1 = f32[12,8,128]{2,1,0:T(8,128)S(1)} collective-permute-done((f32[12,8,128]{2,1,0:T(8,128)S(1)}, f32[12,8,128]{2,1,0:T(8,128)S(1)}, u32[]{:S(2)}, u32[]{:S(2)}) %collective-permute-start.1) | collective-permute-done | bytes 49184 | tf_op jit(solution)/shard_map/ppermute | solution.py:499
  15.0 0.1 shard_map.39.refs_0_
  15.0 5.6 %collective-permute-start.4 = (f32[12,8,128]{2,1,0:T(8,128)S(1)}, f32[12,8,128]{2,1,0:T(8,128)S(1)}, u32[]{:S(2)}, u32[]{:S(2)}) collective-permute-start(f32[12,8,128]{2,1,0:T(8,128)S(1)} %shard_map.39.refs_0_), channel_id=1, source_target_pairs={{0,56},{8,48},{16,40},{24,32},{32,24},{40,16},{48,8},{56,0},{1,57}... | collective-permute-start | bytes 147464 | tf_op jit(solution)/shard_map/ppermute | solution.py:511
  20.6 2.1 %collective-permute-done.4.refs_1_.z4 = f32[12,8,128]{2,1,0:T(8,128)S(1)} collective-permute-done((f32[12,8,128]{2,1,0:T(8,128)S(1)}, f32[12,8,128]{2,1,0:T(8,128)S(1)}, u32[]{:S(2)}, u32[]{:S(2)}) %collective-permute-start.4) | collective-permute-done | bytes 49184 | tf_op jit(solution)/shard_map/ppermute | solution.py:511
  22.7 3.1 %collective-permute-start.7 = (f32[12,8,128]{2,1,0:T(8,128)S(1)}, f32[12,8,128]{2,1,0:T(8,128)S(1)}, u32[]{:S(2)}, u32[]{:S(2)}) collective-permute-start(f32[12,8,128]{2,1,0:T(8,128)S(1)} %shard_map.40), channel_id=1, source_target_pairs={{0,192},{64,128},{128,64},{192,0},{1,193},{65,129},{129,65},{193,1... | collective-permute-start | bytes 147464 | tf_op jit(solution)/shard_map/ppermute | solution.py:499
  25.8 0.6 %collective-permute-start.6 = (f32[12,8,128]{2,1,0:T(8,128)S(1)}, f32[12,8,128]{2,1,0:T(8,128)S(1)}, u32[]{:S(2)}, u32[]{:S(2)}) collective-permute-start(f32[12,8,128]{2,1,0:T(8,128)S(1)} %shard_map.40), channel_id=1, source_target_pairs={{0,128},{64,192},{128,0},{192,64},{1,129},{65,193},{129,1},{193,65... | collective-permute-start | bytes 147464 | tf_op jit(solution)/shard_map/ppermute | solution.py:499
  26.4 2.1 %collective-permute-done.7.y3 = f32[12,8,128]{2,1,0:T(8,128)S(1)} collective-permute-done((f32[12,8,128]{2,1,0:T(8,128)S(1)}, f32[12,8,128]{2,1,0:T(8,128)S(1)}, u32[]{:S(2)}, u32[]{:S(2)}) %collective-permute-start.7) | collective-permute-done | bytes 49184 | tf_op jit(solution)/shard_map/ppermute | solution.py:499
  28.5 0.1 collective-permute-start.5
  28.6 2.8 %collective-permute-done.6.y2 = f32[12,8,128]{2,1,0:T(8,128)S(1)} collective-permute-done((f32[12,8,128]{2,1,0:T(8,128)S(1)}, f32[12,8,128]{2,1,0:T(8,128)S(1)}, u32[]{:S(2)}, u32[]{:S(2)}) %collective-permute-start.6) | collective-permute-done | bytes 49184 | tf_op jit(solution)/shard_map/ppermute | solution.py:499
  31.4 1.2 %collective-permute-done.5.y1 = f32[12,8,128]{2,1,0:T(8,128)S(1)} collective-permute-done((f32[12,8,128]{2,1,0:T(8,128)S(1)}, f32[12,8,128]{2,1,0:T(8,128)S(1)}, u32[]{:S(2)}, u32[]{:S(2)}) %collective-permute-start.5) | collective-permute-done | bytes 49184 | tf_op jit(solution)/shard_map/ppermute | solution.py:499
  32.6 0.2 shard_map.41
  32.8 0.1 collective-permute-start.8
  32.9 3.8 %collective-permute-start.9 = (f32[4,8,128]{2,1,0:T(8,128)S(1)}, f32[4,8,128]{2,1,0:T(8,128)S(1)}, u32[]{:S(2)}, u32[]{:S(2)}) collective-permute-start(f32[4,8,128]{2,1,0:T(8,128)S(1)} %get-tuple-element.24), channel_id=1, source_target_pairs={{0,2},{1,3},{2,0},{3,1},{4,6},{5,7},{6,4},{7,5},{8,10},{9,11},{10,... | collective-permute-start | bytes 49160 | tf_op jit(solution)/shard_map/ppermute | solution.py:499
  36.7 0.9 %collective-permute-start.10 = (f32[4,8,128]{2,1,0:T(8,128)S(1)}, f32[4,8,128]{2,1,0:T(8,128)S(1)}, u32[]{:S(2)}, u32[]{:S(2)}) collective-permute-start(f32[4,8,128]{2,1,0:T(8,128)S(1)} %get-tuple-element.25), channel_id=1, source_target_pairs={{0,3},{1,2},{2,1},{3,0},{4,7},{5,6},{6,5},{7,4},{8,11},{9,10},{10,... | collective-permute-start | bytes 49160 | tf_op jit(solution)/shard_map/ppermute | solution.py:499
  37.6 0.1 shard_map.43.refs_0_
  37.7 0.1 shard_map.44.refs_1_
  37.8 0.1 shard_map.45.refs_2_
  37.9 0.7 %shard_map.46 = (f32[512,128]{1,0:T(8,128)S(1)}, f32[132,8,128]{2,1,0:T(8,128)S(1)}) custom-call(f32[128,128]{1,0:T(8,128)S(1)} %shard_map.43.refs_0_, f32[128,128]{1,0:T(8,128)S(1)} %shard_map.44.refs_1_, f32[128,128]{1,0:T(8,128)S(1)} %shard_map.45.refs_2_, f32[4,128,128]{2,1,0:T(8,128)S(1)} %collective-permute-done.13.refs_3_.refs_7_), custom_call_target="tpu_custom_call" | custom-call | flops 100000 | bytes 1000000 | tf_op jit(solution)/shard_map/pallas_call | solution.py:466
  38.7 3.0 %collective-permute-done.10.refs_3_ = f32[4,8,128]{2,1,0:T(8,128)S(1)} collective-permute-done((f32[4,8,128]{2,1,0:T(8,128)S(1)}, f32[4,8,128]{2,1,0:T(8,128)S(1)}, u32[]{:S(2)}, u32[]{:S(2)}) %collective-permute-start.10) | collective-permute-done | bytes 16416 | tf_op jit(solution)/shard_map/ppermute | solution.py:499
  41.6 1.8 %shard_map.47 = f32[2,16,3584]{2,1,0:T(8,128)} custom-call(f32[4,8,128]{2,1,0:T(8,128)S(1)} %get-tuple-element.22.refs_0_, f32[4,8,128]{2,1,0:T(8,128)S(1)} %collective-permute-done.8.refs_1_, f32[4,8,128]{2,1,0:T(8,128)S(1)} %collective-permute-done.9.refs_2_, f32[4,8,128]{2,1,0:T(8,128)S(1)} %collective-permute-done.10.refs_3_, ...), custom_call_target="tpu_custom_call" | custom-call | flops 100000 | bytes 1000000 | tf_op jit(solution)/shard_map/pallas_call | solution.py:466
  (7 shorter events, 0.1 us)
Async XLA Ops:
  1.5 1.8 %collective-permute-start = (f32[12,8,128]{2,1,0:T(8,128)S(1)}, f32[12,8,128]{2,1,0:T(8,128)S(1)}, u32[]{:S(2)}, u32[]{:S(2)}) collective-permute-start(f32[12,8,128]{2,1,0:T(8,128)S(1)} %get-tuple-element.20.refs_0_.own), channel_id=1, source_target_pairs={{0,4},{4,0},{1,5},{5,1},{2,6},{6,2},{3,7},{7,3},{8,12},{12,8},{9,1... | collective-permute-start | bytes 147464 | tf_op jit(solution)/shard_map/ppermute | solution.py:499
  1.8 34.9 %collective-permute-start.11 = (f32[4,128,128]{2,1,0:T(8,128)S(1)}, f32[4,128,128]{2,1,0:T(8,128)S(1)}, u32[]{:S(2)}, u32[]{:S(2)}) collective-permute-start(f32[4,128,128]{2,1,0:T(8,128)S(1)} %get-tuple-element.30), channel_id=1, source_target_pairs={{0,1},{1,0},{2,3},{3,2},{4,5},{5,4},{6,7},{7,6},{8,9},{9,8},{10,11... | collective-permute-start | bytes 786440 | tf_op jit(solution)/shard_map/ppermute | solution.py:499
  3.4 7.5 %collective-permute-start.3 = (f32[12,8,128]{2,1,0:T(8,128)S(1)}, f32[12,8,128]{2,1,0:T(8,128)S(1)}, u32[]{:S(2)}, u32[]{:S(2)}) collective-permute-start(f32[12,8,128]{2,1,0:T(8,128)S(1)} %shard_map.38.refs_0_), channel_id=1, source_target_pairs={{0,24},{8,16},{16,8},{24,0},{32,56},{40,48},{48,40},{56,32},{1,25}... | collective-permute-start | bytes 147464 | tf_op jit(solution)/shard_map/ppermute | solution.py:499
  5.4 32.4 %collective-permute-start.12 = (f32[4,128,128]{2,1,0:T(8,128)S(1)}, f32[4,128,128]{2,1,0:T(8,128)S(1)}, u32[]{:S(2)}, u32[]{:S(2)}) collective-permute-start(f32[4,128,128]{2,1,0:T(8,128)S(1)} %get-tuple-element.31), channel_id=1, source_target_pairs={{0,2},{1,3},{2,0},{3,1},{4,6},{5,7},{6,4},{7,5},{8,10},{9,11},{10,... | collective-permute-start | bytes 786440 | tf_op jit(solution)/shard_map/ppermute | solution.py:499
  8.1 29.8 %collective-permute-start.13 = (f32[4,128,128]{2,1,0:T(8,128)S(1)}, f32[4,128,128]{2,1,0:T(8,128)S(1)}, u32[]{:S(2)}, u32[]{:S(2)}) collective-permute-start(f32[4,128,128]{2,1,0:T(8,128)S(1)} %get-tuple-element.32), channel_id=1, source_target_pairs={{0,3},{1,2},{2,1},{3,0},{4,7},{5,6},{6,5},{7,4},{8,11},{9,10},{10,... | collective-permute-start | bytes 786440 | tf_op jit(solution)/shard_map/ppermute | solution.py:499
  9.1 5.1 %collective-permute-start.2 = (f32[12,8,128]{2,1,0:T(8,128)S(1)}, f32[12,8,128]{2,1,0:T(8,128)S(1)}, u32[]{:S(2)}, u32[]{:S(2)}) collective-permute-start(f32[12,8,128]{2,1,0:T(8,128)S(1)} %shard_map.38.refs_0_), channel_id=1, source_target_pairs={{0,16},{8,24},{16,0},{24,8},{32,48},{40,56},{48,32},{56,40},{1,17}... | collective-permute-start | bytes 147464 | tf_op jit(solution)/shard_map/ppermute | solution.py:499
  10.9 4.1 %collective-permute-start.1 = (f32[12,8,128]{2,1,0:T(8,128)S(1)}, f32[12,8,128]{2,1,0:T(8,128)S(1)}, u32[]{:S(2)}, u32[]{:S(2)}) collective-permute-start(f32[12,8,128]{2,1,0:T(8,128)S(1)} %shard_map.38.refs_0_), channel_id=1, source_target_pairs={{0,8},{8,0},{16,24},{24,16},{32,40},{40,32},{48,56},{56,48},{1,9},... | collective-permute-start | bytes 147464 | tf_op jit(solution)/shard_map/ppermute | solution.py:499
  15.0 7.6 %collective-permute-start.4 = (f32[12,8,128]{2,1,0:T(8,128)S(1)}, f32[12,8,128]{2,1,0:T(8,128)S(1)}, u32[]{:S(2)}, u32[]{:S(2)}) collective-permute-start(f32[12,8,128]{2,1,0:T(8,128)S(1)} %shard_map.39.refs_0_), channel_id=1, source_target_pairs={{0,56},{8,48},{16,40},{24,32},{32,24},{40,16},{48,8},{56,0},{1,57}... | collective-permute-start | bytes 147464 | tf_op jit(solution)/shard_map/ppermute | solution.py:511
  22.7 5.8 %collective-permute-start.7 = (f32[12,8,128]{2,1,0:T(8,128)S(1)}, f32[12,8,128]{2,1,0:T(8,128)S(1)}, u32[]{:S(2)}, u32[]{:S(2)}) collective-permute-start(f32[12,8,128]{2,1,0:T(8,128)S(1)} %shard_map.40), channel_id=1, source_target_pairs={{0,192},{64,128},{128,64},{192,0},{1,193},{65,129},{129,65},{193,1... | collective-permute-start | bytes 147464 | tf_op jit(solution)/shard_map/ppermute | solution.py:499
  25.8 5.6 %collective-permute-start.6 = (f32[12,8,128]{2,1,0:T(8,128)S(1)}, f32[12,8,128]{2,1,0:T(8,128)S(1)}, u32[]{:S(2)}, u32[]{:S(2)}) collective-permute-start(f32[12,8,128]{2,1,0:T(8,128)S(1)} %shard_map.40), channel_id=1, source_target_pairs={{0,128},{64,192},{128,0},{192,64},{1,129},{65,193},{129,1},{193,65... | collective-permute-start | bytes 147464 | tf_op jit(solution)/shard_map/ppermute | solution.py:499
  28.5 4.1 %collective-permute-start.5 = (f32[12,8,128]{2,1,0:T(8,128)S(1)}, f32[12,8,128]{2,1,0:T(8,128)S(1)}, u32[]{:S(2)}, u32[]{:S(2)}) collective-permute-start(f32[12,8,128]{2,1,0:T(8,128)S(1)} %shard_map.40), channel_id=1, source_target_pairs={{0,64},{64,0},{128,192},{192,128},{1,65},{65,1},{129,193},{193,129... | collective-permute-start | bytes 147464 | tf_op jit(solution)/shard_map/ppermute | solution.py:499
  32.8 5.9 %collective-permute-start.8 = (f32[4,8,128]{2,1,0:T(8,128)S(1)}, f32[4,8,128]{2,1,0:T(8,128)S(1)}, u32[]{:S(2)}, u32[]{:S(2)}) collective-permute-start(f32[4,8,128]{2,1,0:T(8,128)S(1)} %get-tuple-element.23), channel_id=1, source_target_pairs={{0,1},{1,0},{2,3},{3,2},{4,5},{5,4},{6,7},{7,6},{8,9},{9,8},{10,11... | collective-permute-start | bytes 49160 | tf_op jit(solution)/shard_map/ppermute | solution.py:499
  32.9 5.8 %collective-permute-start.9 = (f32[4,8,128]{2,1,0:T(8,128)S(1)}, f32[4,8,128]{2,1,0:T(8,128)S(1)}, u32[]{:S(2)}, u32[]{:S(2)}) collective-permute-start(f32[4,8,128]{2,1,0:T(8,128)S(1)} %get-tuple-element.24), channel_id=1, source_target_pairs={{0,2},{1,3},{2,0},{3,1},{4,6},{5,7},{6,4},{7,5},{8,10},{9,11},{10,... | collective-permute-start | bytes 49160 | tf_op jit(solution)/shard_map/ppermute | solution.py:499
  36.7 5.0 %collective-permute-start.10 = (f32[4,8,128]{2,1,0:T(8,128)S(1)}, f32[4,8,128]{2,1,0:T(8,128)S(1)}, u32[]{:S(2)}, u32[]{:S(2)}) collective-permute-start(f32[4,8,128]{2,1,0:T(8,128)S(1)} %get-tuple-element.25), channel_id=1, source_target_pairs={{0,3},{1,2},{2,1},{3,0},{4,7},{5,6},{6,5},{7,4},{8,11},{9,10},{10,... | collective-permute-start | bytes 49160 | tf_op jit(solution)/shard_map/ppermute | solution.py:499

commit v2 on v1

--- a/solution.py
+++ b/solution.py
@@ -106,14 +106,27 @@
     return [(zero, zero), (one, zero), (zero, zero)], [(one, zero), (zero, zero), (zero, zero)]
 
 
+SPREAD = 7
+
+
 def read(ref):
-    return [(ref[2 * i], ref[2 * i + 1]) for i in range(PARTS // 2)]
+    values = [ref[SUB * i : SUB * (i + 1), :] for i in range(9)] + [ref[pl.ds(SPREAD, SUB, stride=SUB), :]]
+    t00, t10, along, s0, s1 = zip(values[0::2], values[1::2])
+    scale = 1.0 / (t00[0] * t00[0] + t00[1] * t00[1] + t10[0] * t10[0] + t10[1] * t10[1])
+    p, q = mul(along, t00), mul(along, t10)
+    t01 = (p[0] - t10[0] * scale, p[1] + t10[1] * scale)
+    t11 = (q[0] + t00[0] * scale, q[1] - t00[1] * scale)
+    return [t00, t10, t01, t11, s0, s1]
 
 
 def write(ref, span):
-    for i, part in enumerate(span):
-        ref[2 * i] = part[0]
-        ref[2 * i + 1] = part[1]
+    t00, t10, t01, t11, s0, s1 = span
+    scale = 1.0 / (t00[0] * t00[0] + t00[1] * t00[1] + t10[0] * t10[0] + t10[1] * t10[1])
+    along = add(mul((t00[0], -t00[1]), t01), mul((t10[0], -t10[1]), t11))
+    values = [*t00, *t10, *scaled(along, scale), *s0, *s1]
+    for i in range(9):
+        ref[SUB * i : SUB * (i + 1), :] = values[i]
+    ref[pl.ds(SPREAD, SPREAD, stride=SUB), :] = values[9][:SPREAD]
 
 
 def rows(k):
@@ -194,7 +207,7 @@
         march = [march[1], step(c, swing, march[1], march[0], u)]
         waves = [[w[1], step(c, swing, w[1], w[0])] for w in waves]
         if k % (CELLS // 4) == CELLS // 4 - 1 and k < CELLS - 1:
-            write(snap.at[k // (CELLS // 4)], waves[0] + waves[1] + march)
+            write_all(snap.at[k // (CELLS // 4)], 0, waves[0] + waves[1] + march)
     matrix = waves[0] + waves[1]
     write(own, matrix + list(sums_of(matrix, *march)))
     loads[2].wait()
@@ -259,22 +272,23 @@
 
 def close_kernel(own, snap, c1, z1, z2, z3, z4, y1, y2, y3, bound0, bound1, bound2, bound3, bounds):
     x, y, z, c = (lax.axis_index(name) for name in ("xr",) + DEPTH)
-    left, right = ends(own[0])
+    left, right = ends(snap[0, 0])
     left, right = descend_quad(left, right, y, read(y1), read(y2), read(y3))
     left, right = descend_pair(left, right, (z & 4) == 4, read(z4))
     left, right = descend_quad(left, right, z & 3, read(z1), read(z2), read(z3))
     left, right = descend_pair(left, right, c == 1, read(c1))
     right = normal(retreat(right, read(own)))
     v0, v1 = meet(left, right)
+    used = lax.broadcasted_iota(jnp.int32, (SUB, LANE), 0) < SPREAD
     for i in range(4):
         a, b = v0, v1
         if i:
-            span = read(snap.at[i - 1])
+            span = read_all(snap.at[i - 1], 0, 6)
             a, b = through(span[:4], v0, v1)
             a, b = add(a, span[4]), add(b, span[5])
         for j, part in enumerate((a, b)):
-            bounds[i, 2 * j] = MIX.real * part[0] - MIX.imag * part[1]
-            bounds[i, 2 * j + 1] = MIX.real * part[1] + MIX.imag * part[0]
+            bounds[i, 2 * j] = jnp.where(used, MIX.real * part[0] - MIX.imag * part[1], 0.0)
+            bounds[i, 2 * j + 1] = jnp.where(used, MIX.real * part[1] + MIX.imag * part[0], 0.0)
     for d, bound in enumerate((bound0, bound1, bound2, bound3)):
         bound[...] = bounds[x ^ d]
 
@@ -477,7 +491,7 @@
 
 
 def local(sound_field, index_start, index_end):
-    span_shape = shaped(PARTS, SUB, LANE)
+    span_shape = shaped(9 * SUB, LANE)
     cells = SUB * CELLS
     piece = cells // 4
     inputs = (sound_field, index_start, index_end)

time: 43.6 us -> 46.5 us (1.067)
  the two profiles are of different devices: /device:TPU:32 before, /device:TPU:24 now
where the time goes in v2:
time: 46.5 us; the launch traced here: 46.4 us
  starting transfers between devices  22.6 us (49%)
  waiting for transfers between devices  18.8 us (40%)
  Pallas kernels  4.88 us (10%)
    ppermute x13, starting transfers between devices, flip(): lax.ppermute(value, axis, [(i, i ^ d) for i in range(lax.axis_size(axis))])  17.2 us
    ppermute x13, waiting for transfers between devices, flip(): lax.ppermute(value, axis, [(i, i ^ d) for i in range(lax.axis_size(axis))])  16.9 us
    ppermute x1, starting transfers between devices, local(): z4 = lax.ppermute(total, 'z', [(i, 7 - i) for i in range(8)])  5.38 us
    pallas_call x11, Pallas kernels, run(): pl.pallas_call(kernel, out_shape=outs, in_specs=[far if far_in else here]...  4.88 us
    ppermute x1, waiting for transfers between devices, local(): z4 = lax.ppermute(total, 'z', [(i, 7 - i) for i in range(8)])  1.94 us
  transfers between devices with their start and end apart: 14, of which 10 were waited for; matrix products, arithmetic and copies ran while one was open for 0% of the time, Pallas kernels for 3%

profile of v2, /device:TPU:24, one launch (start us, length us, event | category | flops | bytes accessed | tf_op | source)
XLA Modules:
  0.0 46.4 jit_solution(5164961823521208180)
XLA Ops:
  0.0 1.5 %shard_map.37 = (f32[72,128]{1,0:T(8,128)S(1)}, f32[3,12,8,128]{3,2,1,0:T(8,128)S(1)}, f32[2,512,128]{2,1,0:T(8,128)S(1)}, f32[512,128]{1,0:T(8,128)S(1)}, f32[64,896]{1,0:T(8,128)S(1)}) custom-call(f32[2,64,896]{2,1,0:T(8,128)} %field.1, f32[64,896]{1,0:T(8,128)} %start.1, f32[64,896]{1,0:T(8,128)} %end.1), custom_call_target="tpu_custom_call" | custom-call | flops 100000 | bytes 1000000 | tf_op jit(solution)/shard_map/pallas_call | solution.py:480
  1.6 0.1 shard_map.42
  1.7 1.6 %collective-permute-start.11 = (f32[4,128,128]{2,1,0:T(8,128)S(1)}, f32[4,128,128]{2,1,0:T(8,128)S(1)}, u32[]{:S(2)}, u32[]{:S(2)}) collective-permute-start(f32[4,128,128]{2,1,0:T(8,128)S(1)} %get-tuple-element.30), channel_id=1, source_target_pairs={{0,1},{1,0},{2,3},{3,2},{4,5},{5,4},{6,7},{7,6},{8,9},{9,8},{10,11... | collective-permute-start | bytes 786440 | tf_op jit(solution)/shard_map/ppermute | solution.py:513
  3.3 2.7 %collective-permute-start.12 = (f32[4,128,128]{2,1,0:T(8,128)S(1)}, f32[4,128,128]{2,1,0:T(8,128)S(1)}, u32[]{:S(2)}, u32[]{:S(2)}) collective-permute-start(f32[4,128,128]{2,1,0:T(8,128)S(1)} %get-tuple-element.31), channel_id=1, source_target_pairs={{0,2},{1,3},{2,0},{3,1},{4,6},{5,7},{6,4},{7,5},{8,10},{9,11},{10,... | collective-permute-start | bytes 786440 | tf_op jit(solution)/shard_map/ppermute | solution.py:513
  6.0 0.5 %collective-permute-start.13 = (f32[4,128,128]{2,1,0:T(8,128)S(1)}, f32[4,128,128]{2,1,0:T(8,128)S(1)}, u32[]{:S(2)}, u32[]{:S(2)}) collective-permute-start(f32[4,128,128]{2,1,0:T(8,128)S(1)} %get-tuple-element.32), channel_id=1, source_target_pairs={{0,3},{1,2},{2,1},{3,0},{4,7},{5,6},{6,5},{7,4},{8,11},{9,10},{10,... | collective-permute-start | bytes 786440 | tf_op jit(solution)/shard_map/ppermute | solution.py:513
  6.5 1.2 %collective-permute-done.refs_1_.c1 = f32[72,128]{1,0:T(8,128)S(1)} collective-permute-done((f32[72,128]{1,0:T(8,128)S(1)}, f32[72,128]{1,0:T(8,128)S(1)}, u32[]{:S(2)}, u32[]{:S(2)}) %collective-permute-start) | collective-permute-done | bytes 36896 | tf_op jit(solution)/shard_map/ppermute | solution.py:513
  7.7 4.7 %collective-permute-start.3 = (f32[72,128]{1,0:T(8,128)S(1)}, f32[72,128]{1,0:T(8,128)S(1)}, u32[]{:S(2)}, u32[]{:S(2)}) collective-permute-start(f32[72,128]{1,0:T(8,128)S(1)} %shard_map.38.refs_0_), channel_id=1, source_target_pairs={{0,24},{8,16},{16,8},{24,0},{32,56},{40,48},{48,40},{56,32},{1,25}... | collective-permute-start | bytes 110600 | tf_op jit(solution)/shard_map/ppermute | solution.py:513
  12.5 0.0 collective-permute-start.2
  12.5 1.9 %collective-permute-done.3.refs_3_.z3 = f32[72,128]{1,0:T(8,128)S(1)} collective-permute-done((f32[72,128]{1,0:T(8,128)S(1)}, f32[72,128]{1,0:T(8,128)S(1)}, u32[]{:S(2)}, u32[]{:S(2)}) %collective-permute-start.3) | collective-permute-done | bytes 36896 | tf_op jit(solution)/shard_map/ppermute | solution.py:513
  14.4 0.0 collective-permute-start.1
  14.4 3.0 %collective-permute-done.2.refs_2_.z2 = f32[72,128]{1,0:T(8,128)S(1)} collective-permute-done((f32[72,128]{1,0:T(8,128)S(1)}, f32[72,128]{1,0:T(8,128)S(1)}, u32[]{:S(2)}, u32[]{:S(2)}) %collective-permute-start.2) | collective-permute-done | bytes 36896 | tf_op jit(solution)/shard_map/ppermute | solution.py:513
  17.4 1.0 %collective-permute-done.1.refs_1_.z1 = f32[72,128]{1,0:T(8,128)S(1)} collective-permute-done((f32[72,128]{1,0:T(8,128)S(1)}, f32[72,128]{1,0:T(8,128)S(1)}, u32[]{:S(2)}, u32[]{:S(2)}) %collective-permute-start.1) | collective-permute-done | bytes 36896 | tf_op jit(solution)/shard_map/ppermute | solution.py:513
  18.4 0.1 shard_map.39.refs_0_
  18.4 5.4 %collective-permute-start.4 = (f32[72,128]{1,0:T(8,128)S(1)}, f32[72,128]{1,0:T(8,128)S(1)}, u32[]{:S(2)}, u32[]{:S(2)}) collective-permute-start(f32[72,128]{1,0:T(8,128)S(1)} %shard_map.39.refs_0_), channel_id=1, source_target_pairs={{0,56},{8,48},{16,40},{24,32},{32,24},{40,16},{48,8},{56,0},{1,57}... | collective-permute-start | bytes 110600 | tf_op jit(solution)/shard_map/ppermute | solution.py:525
  23.8 1.9 %collective-permute-done.4.refs_1_.z4 = f32[72,128]{1,0:T(8,128)S(1)} collective-permute-done((f32[72,128]{1,0:T(8,128)S(1)}, f32[72,128]{1,0:T(8,128)S(1)}, u32[]{:S(2)}, u32[]{:S(2)}) %collective-permute-start.4) | collective-permute-done | bytes 36896 | tf_op jit(solution)/shard_map/ppermute | solution.py:525
  25.8 0.3 collective-permute-start.7
  26.1 2.6 %collective-permute-start.6 = (f32[72,128]{1,0:T(8,128)S(1)}, f32[72,128]{1,0:T(8,128)S(1)}, u32[]{:S(2)}, u32[]{:S(2)}) collective-permute-start(f32[72,128]{1,0:T(8,128)S(1)} %shard_map.40), channel_id=1, source_target_pairs={{0,128},{64,192},{128,0},{192,64},{1,129},{65,193},{129,1},{193,65... | collective-permute-start | bytes 110600 | tf_op jit(solution)/shard_map/ppermute | solution.py:513
  28.7 2.4 %collective-permute-done.7.y3 = f32[72,128]{1,0:T(8,128)S(1)} collective-permute-done((f32[72,128]{1,0:T(8,128)S(1)}, f32[72,128]{1,0:T(8,128)S(1)}, u32[]{:S(2)}, u32[]{:S(2)}) %collective-permute-start.7) | collective-permute-done | bytes 36896 | tf_op jit(solution)/shard_map/ppermute | solution.py:513
  31.0 0.0 collective-permute-start.5
  31.0 0.5 %collective-permute-done.6.y2 = f32[72,128]{1,0:T(8,128)S(1)} collective-permute-done((f32[72,128]{1,0:T(8,128)S(1)}, f32[72,128]{1,0:T(8,128)S(1)}, u32[]{:S(2)}, u32[]{:S(2)}) %collective-permute-start.6) | collective-permute-done | bytes 36896 | tf_op jit(solution)/shard_map/ppermute | solution.py:513
  31.6 3.4 %collective-permute-done.5.y1 = f32[72,128]{1,0:T(8,128)S(1)} collective-permute-done((f32[72,128]{1,0:T(8,128)S(1)}, f32[72,128]{1,0:T(8,128)S(1)}, u32[]{:S(2)}, u32[]{:S(2)}) %collective-permute-start.5) | collective-permute-done | bytes 36896 | tf_op jit(solution)/shard_map/ppermute | solution.py:513
  35.0 0.2 shard_map.41
  35.2 0.4 collective-permute-start.8
  35.6 4.0 %collective-permute-start.9 = (f32[4,8,128]{2,1,0:T(8,128)S(1)}, f32[4,8,128]{2,1,0:T(8,128)S(1)}, u32[]{:S(2)}, u32[]{:S(2)}) collective-permute-start(f32[4,8,128]{2,1,0:T(8,128)S(1)} %get-tuple-element.24), channel_id=1, source_target_pairs={{0,2},{1,3},{2,0},{3,1},{4,6},{5,7},{6,4},{7,5},{8,10},{9,11},{10,... | collective-permute-start | bytes 49160 | tf_op jit(solution)/shard_map/ppermute | solution.py:513
  39.6 0.4 collective-permute-start.10
  40.0 0.1 shard_map.43.refs_0_
  40.1 0.1 shard_map.44.refs_1_
  40.2 0.1 shard_map.45.refs_2_
  40.3 0.7 %shard_map.46 = (f32[512,128]{1,0:T(8,128)S(1)}, f32[132,8,128]{2,1,0:T(8,128)S(1)}) custom-call(f32[128,128]{1,0:T(8,128)S(1)} %shard_map.43.refs_0_, f32[128,128]{1,0:T(8,128)S(1)} %shard_map.44.refs_1_, f32[128,128]{1,0:T(8,128)S(1)} %shard_map.45.refs_2_, f32[4,128,128]{2,1,0:T(8,128)S(1)} %collective-permute-done.13.refs_3_.refs_7_), custom_call_target="tpu_custom_call" | custom-call | flops 100000 | bytes 1000000 | tf_op jit(solution)/shard_map/pallas_call | solution.py:480
  41.1 0.4 collective-permute-done.9.refs_2_
  41.5 3.1 %collective-permute-done.10.refs_3_ = f32[4,8,128]{2,1,0:T(8,128)S(1)} collective-permute-done((f32[4,8,128]{2,1,0:T(8,128)S(1)}, f32[4,8,128]{2,1,0:T(8,128)S(1)}, u32[]{:S(2)}, u32[]{:S(2)}) %collective-permute-start.10) | collective-permute-done | bytes 16416 | tf_op jit(solution)/shard_map/ppermute | solution.py:513
  44.6 1.8 %shard_map.47 = f32[2,16,3584]{2,1,0:T(8,128)} custom-call(f32[4,8,128]{2,1,0:T(8,128)S(1)} %get-tuple-element.22.refs_0_, f32[4,8,128]{2,1,0:T(8,128)S(1)} %collective-permute-done.8.refs_1_, f32[4,8,128]{2,1,0:T(8,128)S(1)} %collective-permute-done.9.refs_2_, f32[4,8,128]{2,1,0:T(8,128)S(1)} %collective-permute-done.10.refs_3_, ...), custom_call_target="tpu_custom_call" | custom-call | flops 100000 | bytes 1000000 | tf_op jit(solution)/shard_map/pallas_call | solution.py:480
  (7 shorter events, 0.1 us)
Async XLA Ops:
  1.7 37.9 %collective-permute-start.11 = (f32[4,128,128]{2,1,0:T(8,128)S(1)}, f32[4,128,128]{2,1,0:T(8,128)S(1)}, u32[]{:S(2)}, u32[]{:S(2)}) collective-permute-start(f32[4,128,128]{2,1,0:T(8,128)S(1)} %get-tuple-element.30), channel_id=1, source_target_pairs={{0,1},{1,0},{2,3},{3,2},{4,5},{5,4},{6,7},{7,6},{8,9},{9,8},{10,11... | collective-permute-start | bytes 786440 | tf_op jit(solution)/shard_map/ppermute | solution.py:513
  3.3 36.9 %collective-permute-start.12 = (f32[4,128,128]{2,1,0:T(8,128)S(1)}, f32[4,128,128]{2,1,0:T(8,128)S(1)}, u32[]{:S(2)}, u32[]{:S(2)}) collective-permute-start(f32[4,128,128]{2,1,0:T(8,128)S(1)} %get-tuple-element.31), channel_id=1, source_target_pairs={{0,2},{1,3},{2,0},{3,1},{4,6},{5,7},{6,4},{7,5},{8,10},{9,11},{10,... | collective-permute-start | bytes 786440 | tf_op jit(solution)/shard_map/ppermute | solution.py:513
  6.0 34.3 %collective-permute-start.13 = (f32[4,128,128]{2,1,0:T(8,128)S(1)}, f32[4,128,128]{2,1,0:T(8,128)S(1)}, u32[]{:S(2)}, u32[]{:S(2)}) collective-permute-start(f32[4,128,128]{2,1,0:T(8,128)S(1)} %get-tuple-element.32), channel_id=1, source_target_pairs={{0,3},{1,2},{2,1},{3,0},{4,7},{5,6},{6,5},{7,4},{8,11},{9,10},{10,... | collective-permute-start | bytes 786440 | tf_op jit(solution)/shard_map/ppermute | solution.py:513
  6.5 1.2 %collective-permute-start = (f32[72,128]{1,0:T(8,128)S(1)}, f32[72,128]{1,0:T(8,128)S(1)}, u32[]{:S(2)}, u32[]{:S(2)}) collective-permute-start(f32[72,128]{1,0:T(8,128)S(1)} %get-tuple-element.20.refs_0_.own), channel_id=1, source_target_pairs={{0,4},{4,0},{1,5},{5,1},{2,6},{6,2},{3,7},{7,3},{8,12},{12,8},{9,1... | collective-permute-start | bytes 110600 | tf_op jit(solution)/shard_map/ppermute | solution.py:513
  7.7 6.6 %collective-permute-start.3 = (f32[72,128]{1,0:T(8,128)S(1)}, f32[72,128]{1,0:T(8,128)S(1)}, u32[]{:S(2)}, u32[]{:S(2)}) collective-permute-start(f32[72,128]{1,0:T(8,128)S(1)} %shard_map.38.refs_0_), channel_id=1, source_target_pairs={{0,24},{8,16},{16,8},{24,0},{32,56},{40,48},{48,40},{56,32},{1,25}... | collective-permute-start | bytes 110600 | tf_op jit(solution)/shard_map/ppermute | solution.py:513
  12.5 4.9 %collective-permute-start.2 = (f32[72,128]{1,0:T(8,128)S(1)}, f32[72,128]{1,0:T(8,128)S(1)}, u32[]{:S(2)}, u32[]{:S(2)}) collective-permute-start(f32[72,128]{1,0:T(8,128)S(1)} %shard_map.38.refs_0_), channel_id=1, source_target_pairs={{0,16},{8,24},{16,0},{24,8},{32,48},{40,56},{48,32},{56,40},{1,17}... | collective-permute-start | bytes 110600 | tf_op jit(solution)/shard_map/ppermute | solution.py:513
  14.4 4.0 %collective-permute-start.1 = (f32[72,128]{1,0:T(8,128)S(1)}, f32[72,128]{1,0:T(8,128)S(1)}, u32[]{:S(2)}, u32[]{:S(2)}) collective-permute-start(f32[72,128]{1,0:T(8,128)S(1)} %shard_map.38.refs_0_), channel_id=1, source_target_pairs={{0,8},{8,0},{16,24},{24,16},{32,40},{40,32},{48,56},{56,48},{1,9},... | collective-permute-start | bytes 110600 | tf_op jit(solution)/shard_map/ppermute | solution.py:513
  18.4 7.3 %collective-permute-start.4 = (f32[72,128]{1,0:T(8,128)S(1)}, f32[72,128]{1,0:T(8,128)S(1)}, u32[]{:S(2)}, u32[]{:S(2)}) collective-permute-start(f32[72,128]{1,0:T(8,128)S(1)} %shard_map.39.refs_0_), channel_id=1, source_target_pairs={{0,56},{8,48},{16,40},{24,32},{32,24},{40,16},{48,8},{56,0},{1,57}... | collective-permute-start | bytes 110600 | tf_op jit(solution)/shard_map/ppermute | solution.py:525
  25.8 5.3 %collective-permute-start.7 = (f32[72,128]{1,0:T(8,128)S(1)}, f32[72,128]{1,0:T(8,128)S(1)}, u32[]{:S(2)}, u32[]{:S(2)}) collective-permute-start(f32[72,128]{1,0:T(8,128)S(1)} %shard_map.40), channel_id=1, source_target_pairs={{0,192},{64,128},{128,64},{192,0},{1,193},{65,129},{129,65},{193,1... | collective-permute-start | bytes 110600 | tf_op jit(solution)/shard_map/ppermute | solution.py:513
  26.1 5.5 %collective-permute-start.6 = (f32[72,128]{1,0:T(8,128)S(1)}, f32[72,128]{1,0:T(8,128)S(1)}, u32[]{:S(2)}, u32[]{:S(2)}) collective-permute-start(f32[72,128]{1,0:T(8,128)S(1)} %shard_map.40), channel_id=1, source_target_pairs={{0,128},{64,192},{128,0},{192,64},{1,129},{65,193},{129,1},{193,65... | collective-permute-start | bytes 110600 | tf_op jit(solution)/shard_map/ppermute | solution.py:513
  31.0 4.0 %collective-permute-start.5 = (f32[72,128]{1,0:T(8,128)S(1)}, f32[72,128]{1,0:T(8,128)S(1)}, u32[]{:S(2)}, u32[]{:S(2)}) collective-permute-start(f32[72,128]{1,0:T(8,128)S(1)} %shard_map.40), channel_id=1, source_target_pairs={{0,64},{64,0},{128,192},{192,128},{1,65},{65,1},{129,193},{193,129... | collective-permute-start | bytes 110600 | tf_op jit(solution)/shard_map/ppermute | solution.py:513
  35.2 5.9 %collective-permute-start.8 = (f32[4,8,128]{2,1,0:T(8,128)S(1)}, f32[4,8,128]{2,1,0:T(8,128)S(1)}, u32[]{:S(2)}, u32[]{:S(2)}) collective-permute-start(f32[4,8,128]{2,1,0:T(8,128)S(1)} %get-tuple-element.23), channel_id=1, source_target_pairs={{0,1},{1,0},{2,3},{3,2},{4,5},{5,4},{6,7},{7,6},{8,9},{9,8},{10,11... | collective-permute-start | bytes 49160 | tf_op jit(solution)/shard_map/ppermute | solution.py:513
  35.6 5.9 %collective-permute-start.9 = (f32[4,8,128]{2,1,0:T(8,128)S(1)}, f32[4,8,128]{2,1,0:T(8,128)S(1)}, u32[]{:S(2)}, u32[]{:S(2)}) collective-permute-start(f32[4,8,128]{2,1,0:T(8,128)S(1)} %get-tuple-element.24), channel_id=1, source_target_pairs={{0,2},{1,3},{2,0},{3,1},{4,6},{5,7},{6,4},{7,5},{8,10},{9,11},{10,... | collective-permute-start | bytes 49160 | tf_op jit(solution)/shard_map/ppermute | solution.py:513
  39.6 5.0 %collective-permute-start.10 = (f32[4,8,128]{2,1,0:T(8,128)S(1)}, f32[4,8,128]{2,1,0:T(8,128)S(1)}, u32[]{:S(2)}, u32[]{:S(2)}) collective-permute-start(f32[4,8,128]{2,1,0:T(8,128)S(1)} %get-tuple-element.25), channel_id=1, source_target_pairs={{0,3},{1,2},{2,1},{3,0},{4,7},{5,6},{6,5},{7,4},{8,11},{9,10},{10,... | collective-permute-start | bytes 49160 | tf_op jit(solution)/shard_map/ppermute | solution.py:513
